TPU v7x, 256 devices: a whole 4x4x8 slice. The times are simulated.
256 devices in a mesh: slab: 128 (over x, y, z), rhs: 2 (over core).
Axes of the slice: x: 4, y: 4, z: 8, core: 2. Of those that a mesh axis runs over, the one named last changes fastest.
Arguments:
- bond_factor: float32 [128, 2, 256, 256], P('slab'), may hold values from -1 to 2
- tile_mask: int32 [128, 4, 4], P('slab'), may hold values from 0 to 1, as said below
- potential: float32 [128, 256], P('slab'), may hold values from 0.001 to 0.01
- injection: float32 [128, 2, 256, 128], P('slab', None, None, 'rhs'), may hold values from -0.125 to 0.125
Outputs:
- amplitude: float32 [128, 2, 256, 128], P('slab', None, None, 'rhs')
Inputs may be any that keep to these rules, and one draw needn't show every extreme that they name: `tile_mask`: tiles on the diagonal of each slab's tile pattern are 1.
All inputs are finite; a program needn't handle non-finite values.
Results may differ from a plain program's by a relative error of at most 0.0003.
Values sent between devices are 32-bit elements; how exact they have to be, the bound alone decides.
A program may use at most 128 MiB of HBM per device.

v0:
```python
import jax
import jax.numpy as jnp
from jax import lax
from jax.sharding import PartitionSpec as P

PRECISE = lax.Precision.HIGHEST


def passed_along(array, axis, by):
    length = lax.axis_size(axis)
    pairs = [(i, i + by) for i in range(length) if 0 <= i + by < length]
    return lax.ppermute(array, axis, pairs)


def matmul_exact(operand, other):
    return jnp.dot(operand, other, precision=PRECISE)


def transposed_product(operand, other):
    return lax.dot_general(operand, other, (((0,), (0,)), ((), ())), precision=PRECISE)


def complex_product(operand, other):
    real_part = matmul_exact(operand[0], other[0]) - matmul_exact(operand[1], other[1])
    imag_part = matmul_exact(operand[0], other[1]) + matmul_exact(operand[1], other[0])
    return jnp.stack([real_part, imag_part])


def adjoint_product(operand, other):
    real_part = transposed_product(operand[0], other[0]) + transposed_product(operand[1], other[1])
    imag_part = transposed_product(operand[0], other[1]) - transposed_product(operand[1], other[0])
    return jnp.stack([real_part, imag_part])


def adjoint(operand):
    return jnp.stack([operand[0].T, -operand[1].T])


def real_form(matrix):
    return jnp.block([[matrix[0], -matrix[1]], [matrix[1], matrix[0]]])


def solve_stacked(factor_low, stacked):
    forward_part = lax.linalg.triangular_solve(factor_low, stacked, left_side=True, lower=True)
    return lax.linalg.triangular_solve(
        factor_low, forward_part, left_side=True, lower=True, transpose_a=True
    )


def per_device(bond_factor, tile_mask, potential, injection):
    orbitals = bond_factor.shape[2]
    tile_size = orbitals // tile_mask.shape[2]
    slab_total = lax.axis_size("slab")
    position = lax.axis_index("slab")
    core_total = lax.axis_size("rhs")
    core_index = lax.axis_index("rhs")
    half_cols = orbitals // core_total
    pattern = jnp.repeat(jnp.repeat(tile_mask[0], tile_size, 0), tile_size, 1).astype(
        bond_factor.dtype
    )
    factor = bond_factor[0] * pattern[None]
    bond_matrix = complex_product(factor, adjoint(factor))
    previous = passed_along(bond_matrix, "slab", 1)
    onsite = jnp.stack([jnp.diag(potential[0]), jnp.zeros((orbitals, orbitals), potential.dtype)])
    matrix = onsite + bond_matrix + previous
    coupling_up = jnp.where(position == slab_total - 1, jnp.zeros_like(bond_matrix), -bond_matrix)
    coupling_down = -previous
    sources = injection[0]

    def apply_inverse(block, right_side):
        factor_low = jnp.linalg.cholesky(real_form(block))
        stacked = jnp.concatenate([right_side[0], right_side[1]], 0)
        solved = solve_stacked(factor_low, stacked)
        return jnp.stack([solved[:orbitals], solved[orbitals:]])

    def own_columns(block):
        return lax.dynamic_slice_in_dim(block, core_index * half_cols, half_cols, 2)

    levels = slab_total.bit_length() - 1
    for rank_bit in range(levels):
        stride = 1 << rank_bit
        spikes = apply_inverse(
            matrix,
            jnp.concatenate([own_columns(coupling_up), own_columns(coupling_down), sources], 2),
        )
        spike_up = spikes[:, :, :half_cols]
        spike_down = spikes[:, :, half_cols : 2 * half_cols]
        spike_waves = spikes[:, :, 2 * half_cols :]
        toward_upper = adjoint_product(
            coupling_down, jnp.concatenate([spike_down, spike_up, spike_waves], 2)
        )
        from_upper = passed_along(toward_upper, "slab", -stride)
        cross_part = toward_upper[:, :, half_cols : 2 * half_cols]
        toward_lower = adjoint_product(coupling_up, jnp.concatenate([spike_up, spike_waves], 2))
        outgoing = jnp.concatenate(
            [toward_lower[:, :, :half_cols], cross_part, toward_lower[:, :, half_cols:]], 2
        )
        from_lower = passed_along(outgoing, "slab", stride)
        diag_change = from_upper[:, :, :half_cols] + from_lower[:, :, :half_cols]
        new_up = -from_upper[:, :, half_cols : 2 * half_cols]
        coupling_new = from_lower[:, :, half_cols : 2 * half_cols]
        sources = sources - from_upper[:, :, 2 * half_cols :] - from_lower[:, :, 2 * half_cols :]
        gathered = (
            lax.all_gather(diag_change, "rhs", axis=2, tiled=True),
            lax.all_gather(new_up, "rhs", axis=2, tiled=True),
            lax.all_gather(coupling_new, "rhs", axis=2, tiled=True),
        )
        matrix = matrix - gathered[0]
        coupling_up = gathered[1]
        coupling_down = -adjoint(gathered[2])
    amplitude = apply_inverse(matrix, sources)
    return amplitude[None]


def solution(mesh):
    in_specs = (
        P("slab", None, None, None),
        P("slab", None, None),
        P("slab", None),
        P("slab", None, None, "rhs"),
    )
    out_specs = P("slab", None, None, "rhs")
    return jax.shard_map(
        per_device, mesh=mesh, in_specs=in_specs, out_specs=out_specs, check_vma=False
    )
```

profile of v0, /device:TPU:42, one launch (start us, length us, event | category | flops | bytes accessed | tf_op | source)
XLA Modules:
  0.0 1465.7 jit_solution(7407251794152177031)
XLA Ops:
  7.5 11.0 collective-permute-done
  22.6 11.7 cholesky.814
  34.3 9.8 custom-call.65
  46.8 11.7 cholesky.833
  58.5 10.2 custom-call.66
  70.4 11.7 cholesky.854
  94.1 11.7 cholesky.871
  111.0 11.7 while.30
  122.7 39.3 %custom-call.69 = f32[4,128,128]{1,2,0:T(8,128)S(1)} custom-call(f32[4,128,128]{2,1,0:T(8,128)S(1)} %get-tuple-element.105), custom_call_target="InvertDiagBlocksLowerTriangular" | custom-call | tf_op jit(solution)/shard_map/triangular_solve/custom-call.8 | solution.py:45
  201.7 11.7 cholesky.886
  213.6 9.8 custom-call.70
  224.1 11.7 cholesky.905
  237.2 10.2 custom-call.71
  248.1 11.7 cholesky.926
  271.0 11.9 cholesky.943
  294.5 39.3 %custom-call.74 = f32[4,128,128]{1,2,0:T(8,128)S(1)} custom-call(f32[4,128,128]{2,1,0:T(8,128)S(1)} %get-tuple-element.107), custom_call_target="InvertDiagBlocksLowerTriangular" | custom-call | tf_op jit(solution)/shard_map/triangular_solve/custom-call.8 | solution.py:45
  357.6 12.3 collective-permute-done.3
  370.0 21.2 %collective-permute-done.4 = f32[2,256,320]{1,2,0:T(8,128)S(1)} collective-permute-done((f32[2,256,320]{1,2,0:T(8,128)}, f32[2,256,320]{1,2,0:T(8,128)S(1)}, u32[]{:S(2)}, u32[]{:S(2)}) %collective-permute-start.4) | collective-permute-done | bytes 655392 | tf_op jit(solution)/shard_map/ppermute | solution.py:12
  395.4 11.7 cholesky.958
  407.3 9.8 custom-call.75
  417.8 11.7 cholesky.977
  431.0 10.2 custom-call.76
  441.8 11.7 cholesky.998
  464.7 11.9 cholesky.1015
  488.8 39.3 %custom-call.79 = f32[4,128,128]{1,2,0:T(8,128)S(1)} custom-call(f32[4,128,128]{2,1,0:T(8,128)S(1)} %get-tuple-element.109), custom_call_target="InvertDiagBlocksLowerTriangular" | custom-call | tf_op jit(solution)/shard_map/triangular_solve/custom-call.8 | solution.py:45
  555.8 36.3 %collective-permute-done.5 = f32[2,256,320]{1,2,0:T(8,128)S(1)} collective-permute-done((f32[2,256,320]{1,2,0:T(8,128)S(1)}, f32[2,256,320]{1,2,0:T(8,128)S(1)}, u32[]{:S(2)}, u32[]{:S(2)}) %collective-permute-start.5) | collective-permute-done | bytes 655392 | tf_op jit(solution)/shard_map/ppermute | solution.py:12
  592.1 14.0 collective-permute-done.6
  610.3 11.7 cholesky.1030
  622.2 9.8 custom-call.80
  632.7 11.7 cholesky.1049
  645.8 10.2 custom-call.81
  656.7 11.7 cholesky.1070
  679.5 11.9 cholesky.1087
  703.1 39.3 %custom-call.84 = f32[4,128,128]{1,2,0:T(8,128)S(1)} custom-call(f32[4,128,128]{2,1,0:T(8,128)S(1)} %get-tuple-element.111), custom_call_target="InvertDiagBlocksLowerTriangular" | custom-call | tf_op jit(solution)/shard_map/triangular_solve/custom-call.8 | solution.py:45
  769.3 10.6 collective-permute-done.7
  790.2 11.7 cholesky.1102
  802.0 9.8 custom-call.85
  812.5 11.7 cholesky.1121
  825.7 10.2 custom-call.86
  836.6 11.7 cholesky.1142
  859.4 11.9 cholesky.1159
  883.5 39.3 %custom-call.89 = f32[4,128,128]{1,2,0:T(8,128)S(1)} custom-call(f32[4,128,128]{2,1,0:T(8,128)S(1)} %get-tuple-element.113), custom_call_target="InvertDiagBlocksLowerTriangular" | custom-call | tf_op jit(solution)/shard_map/triangular_solve/custom-call.8 | solution.py:45
  948.1 25.2 %collective-permute-done.9 = f32[2,256,320]{1,2,0:T(8,128)S(1)} collective-permute-done((f32[2,256,320]{1,2,0:T(8,128)S(1)}, f32[2,256,320]{1,2,0:T(8,128)S(1)}, u32[]{:S(2)}, u32[]{:S(2)}) %collective-permute-start.9) | collective-permute-done | bytes 655392 | tf_op jit(solution)/shard_map/ppermute | solution.py:12
  977.8 11.7 cholesky.1174
  1000.2 11.7 cholesky.1193
  1013.3 10.2 custom-call.91
  1024.1 11.7 cholesky.1214
  1047.0 11.9 cholesky.1231
  1070.5 39.3 %custom-call.94 = f32[4,128,128]{1,2,0:T(8,128)S(1)} custom-call(f32[4,128,128]{2,1,0:T(8,128)S(1)} %get-tuple-element.115), custom_call_target="InvertDiagBlocksLowerTriangular" | custom-call | tf_op jit(solution)/shard_map/triangular_solve/custom-call.8 | solution.py:45
  1132.8 11.0 collective-permute-done.11
  1152.0 11.7 cholesky.1246
  1174.3 11.7 cholesky.1265
  1187.5 10.2 custom-call.96
  1198.4 11.7 cholesky.1286
  1221.2 11.9 cholesky.1303
  1245.3 39.9 %custom-call.99 = f32[4,128,128]{1,2,0:T(8,128)} custom-call(f32[4,128,128]{2,1,0:T(8,128)S(1)} %get-tuple-element.117), custom_call_target="InvertDiagBlocksLowerTriangular" | custom-call | tf_op jit(solution)/shard_map/triangular_solve/custom-call.8 | solution.py:45
  1310.7 12.0 collective-permute-done.13
  1328.6 11.7 cholesky.1318
  1340.5 9.8 custom-call.100
  1351.0 11.7 cholesky.1337
  1364.1 10.2 custom-call.101
  1374.9 11.7 cholesky.1358
  1397.7 11.9 cholesky.1375
  1421.2 39.3 %custom-call.31 = f32[4,128,128]{1,2,0:T(8,128)S(1)} custom-call(f32[4,128,128]{2,1,0:T(8,128)S(1)} %get-tuple-element.31), custom_call_target="InvertDiagBlocksLowerTriangular" | custom-call | tf_op jit(solution)/shard_map/triangular_solve | solution.py:45
  (750 shorter events, 513.5 us)
Async XLA Ops:
  0.0 1.2 copy-start.33
  3.0 15.6 %collective-permute-start = (f32[2,256,256]{1,2,0:T(8,128)S(1)}, f32[2,256,256]{1,2,0:T(8,128)S(1)}, u32[]{:S(2)}, u32[]{:S(2)}) collective-permute-start(f32[2,256,256]{1,2,0:T(8,128)S(1)} %pad_maximum_fusion.21), channel_id=1, source_target_pairs={{0,2},{2,4},{4,6},{6,8},{8,10},{10,12},{12,14},{14,16},{16,18},{18... | collective-permute-start | bytes 1572872 | tf_op jit(solution)/shard_map/ppermute | solution.py:12
  6.8 0.7 copy-start.37
  21.6 1.0 copy-start.1
  162.0 0.9 copy-start.34
  163.0 1.2 copy-start
  172.0 19.4 %collective-permute-start.1 = (f32[2,256,320]{1,2,0:T(8,128)S(1)}, f32[2,256,320]{1,2,0:T(8,128)S(1)}, u32[]{:S(2)}, u32[]{:S(2)}) collective-permute-start(f32[2,256,320]{1,2,0:T(8,128)S(1)} %pad_maximum_fusion.3), channel_id=1, source_target_pairs={{2,0},{4,2},{6,4},{8,6},{10,8},{12,10},{14,12},{16,14},{18,16},{20... | collective-permute-start | bytes 1966088 | tf_op jit(solution)/shard_map/ppermute | solution.py:12
  179.8 17.7 %collective-permute-start.2 = (f32[2,256,320]{1,2,0:T(8,128)}, f32[2,256,320]{1,2,0:T(8,128)S(1)}, u32[]{:S(2)}, u32[]{:S(2)}) collective-permute-start(f32[2,256,320]{1,2,0:T(8,128)} %fusion.44), channel_id=1, source_target_pairs={{0,2},{2,4},{4,6},{6,8},{8,10},{10,12},{12,14},{14,16},{16,18},{18... | collective-permute-start | bytes 1966088 | tf_op jit(solution)/shard_map/ppermute | solution.py:12
  191.4 7.1 copy-start.23
  197.5 1.0 copy-start.29
  286.3 47.5 %copy-start.17 = (f32[2,256,128]{1,2,0:T(8,128)S(1)}, f32[2,256,128]{1,2,0:T(8,128)}, u32[]{:S(2)}) copy-start(f32[2,256,128]{1,2,0:T(8,128)} %get-tuple-element.237) | copy-start | bytes 786436
  336.2 1.0 copy-start.8
  340.3 0.7 copy-start.6
  349.1 20.9 %collective-permute-start.3 = (f32[2,256,320]{1,2,0:T(8,128)S(1)}, f32[2,256,320]{1,2,0:T(8,128)S(1)}, u32[]{:S(2)}, u32[]{:S(2)}) collective-permute-start(f32[2,256,320]{1,2,0:T(8,128)S(1)} %pad_maximum_fusion.4), channel_id=1, source_target_pairs={{4,0},{6,2},{8,4},{10,6},{12,8},{14,10},{16,12},{18,14},{20,16},{2... | collective-permute-start | bytes 1966088 | tf_op jit(solution)/shard_map/ppermute | solution.py:12
  355.4 35.8 %collective-permute-start.4 = (f32[2,256,320]{1,2,0:T(8,128)}, f32[2,256,320]{1,2,0:T(8,128)S(1)}, u32[]{:S(2)}, u32[]{:S(2)}) collective-permute-start(f32[2,256,320]{1,2,0:T(8,128)} %fusion.43), channel_id=1, source_target_pairs={{0,4},{2,6},{4,8},{6,10},{8,12},{10,14},{12,16},{14,18},{16,20},{1... | collective-permute-start | bytes 1966088 | tf_op jit(solution)/shard_map/ppermute | solution.py:12
  370.0 22.2 %copy-start.24 = (f32[2,256,320]{1,2,0:T(8,128)}, f32[2,256,320]{1,2,0:T(8,128)S(1)}, u32[]{:S(2)}) copy-start(f32[2,256,320]{1,2,0:T(8,128)S(1)} %collective-permute-done.3) | copy-start | bytes 1966084
  391.2 1.0 copy-start.30
  480.1 48.0 %copy-start.11 = (f32[2,256,128]{1,2,0:T(8,128)S(1)}, f32[2,256,128]{1,2,0:T(8,128)}, u32[]{:S(2)}) copy-start(f32[2,256,128]{1,2,0:T(8,128)} %get-tuple-element.230) | copy-start | bytes 786436
  530.4 0.9 copy-start.7
  532.3 1.0 copy-start.14
  544.4 47.7 %collective-permute-start.5 = (f32[2,256,320]{1,2,0:T(8,128)S(1)}, f32[2,256,320]{1,2,0:T(8,128)S(1)}, u32[]{:S(2)}, u32[]{:S(2)}) collective-permute-start(f32[2,256,320]{1,2,0:T(8,128)S(1)} %pad_maximum_fusion.5), channel_id=1, source_target_pairs={{8,0},{10,2},{12,4},{14,6},{16,8},{18,10},{20,12},{22,14},{24,16},... | collective-permute-start | bytes 1966088 | tf_op jit(solution)/shard_map/ppermute | solution.py:12
  548.0 58.1 %collective-permute-start.6 = (f32[2,256,320]{1,2,0:T(8,128)}, f32[2,256,320]{1,2,0:T(8,128)S(1)}, u32[]{:S(2)}, u32[]{:S(2)}) collective-permute-start(f32[2,256,320]{1,2,0:T(8,128)} %fusion.42), channel_id=1, source_target_pairs={{0,8},{2,10},{4,12},{6,14},{8,16},{10,18},{12,20},{14,22},{16,24},... | collective-permute-start | bytes 1966088 | tf_op jit(solution)/shard_map/ppermute | solution.py:12
  592.1 15.0 %copy-start.21 = (f32[2,256,320]{1,2,0:T(8,128)}, f32[2,256,320]{1,2,0:T(8,128)S(1)}, u32[]{:S(2)}) copy-start(f32[2,256,320]{1,2,0:T(8,128)S(1)} %collective-permute-done.5) | copy-start | bytes 1966084
  606.1 1.0 copy-start.27
  694.8 47.5 %copy-start.18 = (f32[2,256,128]{1,2,0:T(8,128)S(1)}, f32[2,256,128]{1,2,0:T(8,128)}, u32[]{:S(2)}) copy-start(f32[2,256,128]{1,2,0:T(8,128)} %get-tuple-element.225) | copy-start | bytes 786436
  744.8 1.0 copy-start.9
  748.9 0.7 copy-start.2
  757.7 22.1 %collective-permute-start.7 = (f32[2,256,320]{1,2,0:T(8,128)S(1)}, f32[2,256,320]{1,2,0:T(8,128)S(1)}, u32[]{:S(2)}, u32[]{:S(2)}) collective-permute-start(f32[2,256,320]{1,2,0:T(8,128)S(1)} %pad_maximum_fusion.6), channel_id=1, source_target_pairs={{16,0},{18,2},{20,4},{22,6},{24,8},{26,10},{28,12},{30,14},{32,16}... | collective-permute-start | bytes 1966088 | tf_op jit(solution)/shard_map/ppermute | solution.py:12
  767.3 18.6 %collective-permute-start.8 = (f32[2,256,320]{1,2,0:T(8,128)}, f32[2,256,320]{1,2,0:T(8,128)S(1)}, u32[]{:S(2)}, u32[]{:S(2)}) collective-permute-start(f32[2,256,320]{1,2,0:T(8,128)} %fusion.41), channel_id=1, source_target_pairs={{0,16},{2,18},{4,20},{6,22},{8,24},{10,26},{12,28},{14,30},{16,32}... | collective-permute-start | bytes 1966088 | tf_op jit(solution)/shard_map/ppermute | solution.py:12
  779.8 7.1 copy-start.25
  785.9 1.0 copy-start.31
  874.8 48.0 %copy-start.12 = (f32[2,256,128]{1,2,0:T(8,128)S(1)}, f32[2,256,128]{1,2,0:T(8,128)}, u32[]{:S(2)}) copy-start(f32[2,256,128]{1,2,0:T(8,128)} %get-tuple-element.218) | copy-start | bytes 786436
  925.1 0.9 copy-start.3
  927.0 1.0 copy-start.15
  939.2 34.2 %collective-permute-start.9 = (f32[2,256,320]{1,2,0:T(8,128)S(1)}, f32[2,256,320]{1,2,0:T(8,128)S(1)}, u32[]{:S(2)}, u32[]{:S(2)}) collective-permute-start(f32[2,256,320]{1,2,0:T(8,128)S(1)} %pad_maximum_fusion.7), channel_id=1, source_target_pairs={{32,0},{34,2},{36,4},{38,6},{40,8},{42,10},{44,12},{46,14},{48,16}... | collective-permute-start | bytes 1966088 | tf_op jit(solution)/shard_map/ppermute | solution.py:12
  943.6 29.8 %collective-permute-start.10 = (f32[2,256,320]{1,2,0:T(8,128)}, f32[2,256,320]{1,2,0:T(8,128)S(1)}, u32[]{:S(2)}, u32[]{:S(2)}) collective-permute-start(f32[2,256,320]{1,2,0:T(8,128)} %fusion.40), channel_id=1, source_target_pairs={{0,32},{2,34},{4,36},{6,38},{8,40},{10,42},{12,44},{14,46},{16,48}... | collective-permute-start | bytes 1966088 | tf_op jit(solution)/shard_map/ppermute | solution.py:12
  973.4 1.0 copy-start.22
  973.4 1.2 copy-start.28
  1062.3 47.5 %copy-start.19 = (f32[2,256,128]{1,2,0:T(8,128)S(1)}, f32[2,256,128]{1,2,0:T(8,128)}, u32[]{:S(2)}) copy-start(f32[2,256,128]{1,2,0:T(8,128)} %get-tuple-element.213) | copy-start | bytes 786436
  1112.3 1.0 copy-start.10
  1116.4 0.7 copy-start.4
  1125.1 18.7 %collective-permute-start.11 = (f32[2,256,320]{1,2,0:T(8,128)S(1)}, f32[2,256,320]{1,2,0:T(8,128)S(1)}, u32[]{:S(2)}, u32[]{:S(2)}) collective-permute-start(f32[2,256,320]{1,2,0:T(8,128)S(1)} %pad_maximum_fusion.8), channel_id=1, source_target_pairs={{64,0},{66,2},{68,4},{70,6},{72,8},{74,10},{76,12},{78,14},{80,16}... | collective-permute-start | bytes 1966088 | tf_op jit(solution)/shard_map/ppermute | solution.py:12
  1128.9 18.9 %collective-permute-start.12 = (f32[2,256,320]{1,2,0:T(8,128)}, f32[2,256,320]{1,2,0:T(8,128)S(1)}, u32[]{:S(2)}, u32[]{:S(2)}) collective-permute-start(f32[2,256,320]{1,2,0:T(8,128)} %fusion.39), channel_id=1, source_target_pairs={{0,64},{2,66},{4,68},{6,70},{8,72},{10,74},{12,76},{14,78},{16,80}... | collective-permute-start | bytes 1966088 | tf_op jit(solution)/shard_map/ppermute | solution.py:12
  1143.8 4.9 copy-start.26
  1147.7 1.0 copy-start.32
  1236.7 48.6 %copy-start.13 = (f32[2,256,128]{1,2,0:T(8,128)S(1)}, f32[2,256,128]{1,2,0:T(8,128)}, u32[]{:S(2)}) copy-start(f32[2,256,128]{1,2,0:T(8,128)} %get-tuple-element.206) | copy-start | bytes 786436
  1287.5 0.9 copy-start.5
  1289.4 1.0 copy-start.16
  1292.8 1.0 copy-start.20
  1302.5 20.2 %collective-permute-start.13 = (f32[2,256,320]{1,2,0:T(8,128)S(1)}, f32[2,256,320]{1,2,0:T(8,128)S(1)}, u32[]{:S(2)}, u32[]{:S(2)}) collective-permute-start(f32[2,256,320]{1,2,0:T(8,128)S(1)} %pad_maximum_fusion.9), channel_id=1, source_target_pairs={{128,0},{130,2},{132,4},{134,6},{136,8},{138,10},{140,12},{142,14}... | collective-permute-start | bytes 1966088 | tf_op jit(solution)/shard_map/ppermute | solution.py:12
  1304.5 20.1 %collective-permute-start.14 = (f32[2,256,320]{1,2,0:T(8,128)S(1)}, f32[2,256,320]{1,2,0:T(8,128)S(1)}, u32[]{:S(2)}, u32[]{:S(2)}) collective-permute-start(f32[2,256,320]{1,2,0:T(8,128)S(1)} %fusion.38), channel_id=1, source_target_pairs={{0,128},{2,130},{4,132},{6,134},{8,136},{10,138},{12,140},{14,142}... | collective-permute-start | bytes 1966088 | tf_op jit(solution)/shard_map/ppermute | solution.py:12
  1322.6 5.2 copy-start.35
  1324.6 0.8 copy-start.36
where the time goes:
time: 1480 us; the launch traced here: 1470 us
  other arithmetic  981 us (66%)
  waiting for transfers between devices  181 us (12%)
  local copies, waits for them, and re-layouts  92 us (6%)
  matrix products  84.3 us (6%)
  starting transfers between devices  58.6 us (4%)
  blocking collectives  42.8 us (3%)
  between operations  25 us (2%)
    another operation x119, other arithmetic, apply_inverse(): factor_low = jnp.linalg.cholesky(real_form(block))  637 us
    another operation x17, other arithmetic, solve_stacked(): lax.linalg.triangular_solve(factor_low, forward_part, left_side=True, low...  317 us
    ppermute x15, waiting for transfers between devices, passed_along(): return lax.ppermute(array, axis, pairs)  181 us
    another operation x93, local copies, waits for them, and re-layouts, solve_stacked(): lax.linalg.triangular_solve(factor_low, forward_part, left_side=True, low...  61.6 us
    ppermute x15, starting transfers between devices, passed_along(): return lax.ppermute(array, axis, pairs)  58.6 us
  transfers between devices with their start and end apart: 15, of which 14 were waited for; matrix products, arithmetic and copies ran while one was open for 1% of the time, Pallas kernels for 0%

commit v1 on v0

--- a/solution.py
+++ b/solution.py
@@ -1,9 +1,17 @@
+import functools
+
 import jax
 import jax.numpy as jnp
 from jax import lax
+from jax.experimental import pallas as pl
+from jax.experimental.pallas import tpu as pltpu
 from jax.sharding import PartitionSpec as P
 
 PRECISE = lax.Precision.HIGHEST
+MESH = pl.DeviceIdType.MESH
+F32 = jnp.float32
+BF16 = jnp.bfloat16
+RESIDUAL_LIMIT = 4.0e-4
 
 
 def passed_along(array, axis, by):
@@ -47,7 +55,7 @@
     )
 
 
-def per_device(bond_factor, tile_mask, potential, injection):
+def direct_path(bond_factor, tile_mask, potential, injection):
     orbitals = bond_factor.shape[2]
     tile_size = orbitals // tile_mask.shape[2]
     slab_total = lax.axis_size("slab")
@@ -112,6 +120,450 @@
     return amplitude[None]
 
 
+def split(value):
+    high = value.astype(BF16)
+    low = (value - high.astype(F32)).astype(BF16)
+    return high, low
+
+
+def dot(left, right):
+    return jnp.dot(left, right, preferred_element_type=F32)
+
+
+def dot3(left, right):
+    high = dot(left[0], right[0])
+    return high + (dot(left[0], right[1]) + dot(left[1], right[0]))
+
+
+def pair_map(function, pair):
+    return function(pair[0]), function(pair[1])
+
+
+def tree_kernel(
+    slabs,
+    factor_ref,
+    mask_ref,
+    potential_ref,
+    injection_ref,
+    out_ref,
+    flag_ref,
+    ground,
+    coupling,
+    waves,
+    flag,
+    bond_out,
+    near_bond,
+    near_out,
+    far_out,
+    terms_in,
+    wave_in,
+    wave_out,
+    back,
+    send_sem,
+    bond_sem,
+    terms_sem,
+    wave_sem,
+    wave_send_sem,
+    join_send_sem,
+    join_sem,
+):
+    size = factor_ref.shape[2]
+    half = size // 2
+    cols = injection_ref.shape[3]
+    tile = size // mask_ref.shape[2]
+    position = lax.axis_index("slab")
+    core = lax.axis_index("rhs")
+    twin = 1 - core
+    levels = slabs.bit_length() - 1
+
+    level = jnp.int32(0)
+    stride = jnp.int32(1)
+    for k in range(1, levels + 1):
+        even = jnp.where(position % (1 << k) == 0, 1, 0)
+        level = level + even
+        stride = stride + even * (1 << (k - 1))
+    is_root = position == 0
+    not_root = position > 0
+    has_right = jnp.logical_and(not_root, position + stride < slabs)
+    near_is_right = jnp.logical_and(has_right, (position // stride) % 4 == 1)
+    near = jnp.where(near_is_right, 1, 0)
+    far = 1 - near
+    near_target = jnp.where(near_is_right, position + stride, position - stride)
+    far_target = jnp.where(near_is_right, position - stride, position + stride)
+
+    def remote(source, target, sent, received, slab_to, core_to):
+        return pltpu.make_async_remote_copy(
+            src_ref=source,
+            dst_ref=target,
+            send_sem=sent,
+            recv_sem=received,
+            device_id=(slab_to, core_to),
+            device_id_type=MESH,
+        )
+
+    barrier = pltpu.get_barrier_semaphore()
+
+    def greet(slab_to, core_to):
+        pl.semaphore_signal(barrier, inc=1, device_id=(slab_to, core_to), device_id_type=MESH)
+
+    greet(position, twin)
+    for k in range(levels):
+        step = 1 << k
+        pl.when(jnp.logical_and(level >= k, position + step < slabs))(
+            functools.partial(greet, position + step, core)
+        )
+        pl.when(jnp.logical_and(level >= k, position >= step))(
+            functools.partial(greet, position - step, core)
+        )
+
+    lane = lax.broadcasted_iota(jnp.int32, (1, 128), 1)
+    masked = []
+    for plane in range(2):
+        rows = []
+        for r in range(size // tile):
+            blocks = []
+            for k in range(size // 128):
+                keep = mask_ref[0, r, k * 128 // tile].astype(F32)
+                for t in range(1, 128 // tile):
+                    other = mask_ref[0, r, k * 128 // tile + t].astype(F32)
+                    keep = jnp.where(lane >= t * tile, other, keep)
+                piece = factor_ref[0, plane, r * tile : (r + 1) * tile, k * 128 : (k + 1) * 128]
+                blocks.append(piece * keep)
+            rows.append(jnp.concatenate(blocks, 1))
+        masked.append(jnp.concatenate(rows, 0))
+    left = split(jnp.concatenate(masked, 1))
+    turned = [masked[0].T, -masked[1].T]
+    right = pair_map(
+        lambda planes: planes,
+        split(
+            jnp.concatenate(
+                [jnp.concatenate(turned, 1), jnp.concatenate([-turned[1], turned[0]], 1)], 0
+            )
+        ),
+    )
+    bond = dot3(left, right)
+
+    def store_halves(store, value):
+        for h in range(2):
+            for plane in range(2):
+                store(h, plane, value[:, plane * size + h * half : plane * size + (h + 1) * half])
+
+    def keep_out(h, plane, value):
+        bond_out[h, plane] = value
+
+    store_halves(keep_out, bond)
+
+    row = lax.broadcasted_iota(jnp.int32, (size, half), 0)
+    column = lax.broadcasted_iota(jnp.int32, (size, half), 1) + core * half
+    own = jnp.where(
+        core == 0, potential_ref[:, 0:half], potential_ref[:, half:size]
+    )
+    ground[core, 0] = jnp.where(row == column, jnp.broadcast_to(own, (size, half)), 0.0)
+    ground[core, 1] = jnp.zeros((size, half), F32)
+    waves[...] = jnp.concatenate([injection_ref[0, 0], injection_ref[0, 1]], 1)
+    flag[...] = jnp.zeros_like(flag)
+
+    @pl.when(jnp.logical_not(has_right))
+    def _():
+        coupling[1] = jnp.zeros((2, 2, size, half), F32)
+
+    @pl.when(is_root)
+    def _():
+        coupling[0] = jnp.zeros((2, 2, size, half), F32)
+
+    @pl.when(position == slabs - 1)
+    def _():
+        ground[core] = ground[core] + bond_out[core]
+
+    @pl.when(jnp.logical_and(level == 0, has_right))
+    def _():
+        coupling[1] = bond_out[...]
+
+    partners = jnp.int32(1)
+    for k in range(levels):
+        step = 1 << k
+        partners += jnp.where(jnp.logical_and(level >= k, position + step < slabs), 1, 0)
+        partners += jnp.where(jnp.logical_and(level >= k, position >= step), 1, 0)
+    pl.semaphore_wait(barrier, partners)
+
+    def bond_copy():
+        return remote(
+            bond_out.at[core],
+            coupling.at[0, core],
+            send_sem.at[0],
+            bond_sem.at[0],
+            position + 1,
+            core,
+        )
+
+    pl.when(level > 0)(lambda: bond_copy().start())
+
+    def terms_arrival(k, side):
+        return remote(
+            terms_in.at[k, side], terms_in.at[k, side], send_sem.at[1], terms_sem.at[k, side], position, twin
+        )
+
+    def add_terms(k, side):
+        terms_arrival(k, side).wait_recv()
+        ground[core, 0] += terms_in[k, side, 0:size]
+        ground[core, 1] += terms_in[k, side, size : 2 * size]
+        waves[...] += terms_in[k, side, 2 * size : 3 * size]
+        flag[...] = jnp.maximum(flag[...], terms_in[k, side, 3 * size : 3 * size + 8])
+
+    def add_level(k):
+        pl.when(not_root)(functools.partial(add_terms, k, 0))
+        add_terms(k, 1)
+
+    @pl.loop(0, jnp.maximum(level - 1, 0))
+    def _(k):
+        add_level(k)
+
+    def join(block, which):
+        return remote(block, block, join_send_sem.at[which], join_sem.at[which], position, twin)
+
+    @pl.when(not_root)
+    def _():
+        remote(
+            coupling.at[0, core], coupling.at[0, core], send_sem.at[1], bond_sem.at[0], position, twin
+        ).wait_recv()
+        join(coupling.at[0, core], 0).start()
+
+    two_sided = jnp.logical_and(level > 0, has_right)
+
+    @pl.when(two_sided)
+    def _():
+        remote(
+            coupling.at[1, core], coupling.at[1, core], send_sem.at[1], bond_sem.at[1], position, twin
+        ).wait_recv()
+        join(coupling.at[1, core], 1).start()
+
+    pl.when(level > 0)(lambda: add_level(level - 1))
+    join(ground.at[core], 2).start()
+    pl.when(not_root)(lambda: join(coupling.at[0, twin], 0).wait_recv())
+    pl.when(two_sided)(lambda: join(coupling.at[1, twin], 1).wait_recv())
+    join(ground.at[twin], 2).wait_recv()
+
+    def whole(block):
+        return jnp.concatenate([block[0, 0], block[1, 0], block[0, 1], block[1, 1]], 1)
+
+    def turn(value):
+        width = value.shape[1] // 2
+        return jnp.concatenate([-value[:, width:], value[:, :width]], 1)
+
+    def expand(value):
+        return jnp.concatenate([value, turn(value)], 0)
+
+    matrix = whole(ground) + whole(coupling.at[0]) + whole(coupling.at[1])
+    wide_row = lax.broadcasted_iota(jnp.int32, (size, 2 * size), 0)
+    wide_column = lax.broadcasted_iota(jnp.int32, (size, 2 * size), 1)
+    unit = jnp.where(wide_row == wide_column, 1.0, 0.0).astype(F32)
+    mean = jnp.sum(matrix * unit, keepdims=True) / size
+    scale = 1.0 / mean
+    scaled = matrix * scale
+    power = unit - scaled
+    inverse = unit + power
+    power = power.astype(BF16)
+    power = dot(power, expand(power)).astype(BF16)
+    for k in range(3):
+        both = dot(jnp.concatenate([inverse.astype(BF16), power], 0), expand(power))
+        inverse = inverse + both[:size]
+        power = both[size:].astype(BF16)
+    inverse = inverse + dot(inverse.astype(BF16), expand(power))
+    residual = unit - dot3(split(scaled), pair_map(expand, split(inverse)))
+    inverse = inverse + dot(inverse.astype(BF16), expand(residual.astype(BF16)))
+    squared = jnp.sum(residual * residual, keepdims=True)
+    bad = jnp.where(squared < RESIDUAL_LIMIT, 0.0, 1.0)
+    flag[...] = jnp.maximum(flag[...], jnp.broadcast_to(bad, (8, 128)))
+    solver = split(inverse * scale)
+
+    def turn_waves(value):
+        return jnp.concatenate([-value[:, cols:], value[:, :cols]], 1)
+
+    def expand_waves(value):
+        return jnp.concatenate([value, turn_waves(value)], 0)
+
+    solved_waves = dot3(solver, pair_map(expand_waves, split(waves[...])))
+
+    def own_half(block):
+        return jnp.concatenate([block[core, 0], block[core, 1]], 1)
+
+    near_copy_bond = remote(
+        near_bond,
+        coupling.at[far, core],
+        send_sem.at[2],
+        bond_sem.at[far],
+        near_target,
+        core,
+    )
+    near_copy = remote(
+        near_out,
+        terms_in.at[level, far],
+        send_sem.at[3],
+        terms_sem.at[level, far],
+        near_target,
+        core,
+    )
+    far_copy = remote(
+        far_out,
+        terms_in.at[level, near],
+        send_sem.at[4],
+        terms_sem.at[level, near],
+        far_target,
+        core,
+    )
+
+    @pl.when(not_root)
+    def _():
+        def adjoint_pair(block):
+            real = jnp.concatenate([block[0, 0], block[1, 0]], 1).T
+            imag = jnp.concatenate([block[0, 1], block[1, 1]], 1).T
+            return split(jnp.concatenate([real, -imag], 1))
+
+        near_left = adjoint_pair(coupling.at[near])
+
+        @pl.when(has_right)
+        def _():
+            solved = dot3(solver, pair_map(expand, split(own_half(coupling.at[far]))))
+            product = dot3(near_left, pair_map(expand, split(solved)))
+            near_bond[0] = product[:, :half]
+            near_bond[1] = product[:, half:]
+            near_copy_bond.start()
+
+        solved_ground = pair_map(expand, split(dot3(solver, pair_map(expand, split(own_half(ground))))))
+        waves_pair = pair_map(expand_waves, split(solved_waves))
+
+        def fill(out, left_pair):
+            product = dot3(left_pair, solved_ground)
+            out[0:size] = product[:, :half]
+            out[size : 2 * size] = product[:, half:]
+            out[2 * size : 3 * size] = dot3(left_pair, waves_pair)
+            out[3 * size : 3 * size + 8] = flag[...]
+
+        fill(near_out, near_left)
+        near_copy.start()
+
+        @pl.when(has_right)
+        def _():
+            fill(far_out, adjoint_pair(coupling.at[far]))
+            far_copy.start()
+
+        for side in range(2):
+            spike = split(dot3(solver, pair_map(expand, split(whole(coupling.at[side])))))
+            for part in range(2):
+                back[part, :, side * 2 * size : (side + 1) * 2 * size] = spike[part]
+
+    def wave_arrival(side):
+        return remote(
+            wave_in.at[side], wave_in.at[side], send_sem.at[1], wave_sem.at[side], position, twin
+        )
+
+    wave_out[0:size] = solved_waves
+
+    @pl.when(not_root)
+    def _():
+        def add_side(side):
+            wave_arrival(side).wait_recv()
+            pair = pair_map(expand_waves, split(wave_in[side, 0:size]))
+            spike = (
+                back[0, :, side * 2 * size : (side + 1) * 2 * size],
+                back[1, :, side * 2 * size : (side + 1) * 2 * size],
+            )
+            wave_out[0:size] += dot3(spike, pair)
+
+        add_side(0)
+        flag[...] = jnp.maximum(flag[...], wave_in[0, size : size + 8])
+        pl.when(has_right)(functools.partial(add_side, 1))
+
+    wave_out[size : size + 8] = flag[...]
+
+    @pl.loop(0, level)
+    def _(down):
+        k = level - 1 - down
+        step = jnp.int32(1)
+        for m in range(1, levels):
+            step = step + jnp.where(k >= m, 1 << (m - 1), 0)
+        to_right = remote(
+            wave_out, wave_in.at[0], wave_send_sem.at[0], wave_sem.at[0], position + step, core
+        )
+        to_left = remote(
+            wave_out, wave_in.at[1], wave_send_sem.at[1], wave_sem.at[1], position - step, core
+        )
+        to_right.start()
+        pl.when(not_root)(lambda: to_left.start())
+        to_right.wait_send()
+        pl.when(not_root)(lambda: to_left.wait_send())
+
+    out_ref[0, 0] = wave_out[0:size, :cols]
+    out_ref[0, 1] = wave_out[0:size, cols:]
+    flag_ref[...] = flag[...]
+
+    pl.when(level > 0)(lambda: bond_copy().wait_send())
+    pl.when(not_root)(lambda: join(coupling.at[0, core], 0).wait_send())
+    pl.when(two_sided)(lambda: join(coupling.at[1, core], 1).wait_send())
+    join(ground.at[core], 2).wait_send()
+    pl.when(not_root)(lambda: near_copy.wait_send())
+
+    @pl.when(has_right)
+    def _():
+        near_copy_bond.wait_send()
+        far_copy.wait_send()
+
+
+def tree_path(slabs, bond_factor, tile_mask, potential, injection):
+    size = bond_factor.shape[2]
+    half = size // 2
+    levels = slabs.bit_length() - 1
+    vmem = pl.BlockSpec(memory_space=pltpu.VMEM)
+    rows = 3 * size + 8
+    return pl.pallas_call(
+        functools.partial(tree_kernel, slabs),
+        out_shape=(
+            jax.ShapeDtypeStruct(injection.shape, F32),
+            jax.ShapeDtypeStruct((8, 128), F32),
+        ),
+        in_specs=[vmem, pl.BlockSpec(memory_space=pltpu.SMEM), vmem, vmem],
+        out_specs=(vmem, vmem),
+        scratch_shapes=[
+            pltpu.VMEM((2, 2, size, half), F32),
+            pltpu.VMEM((2, 2, 2, size, half), F32),
+            pltpu.VMEM((size, 128), F32),
+            pltpu.VMEM((8, 128), F32),
+            pltpu.VMEM((2, 2, size, half), F32),
+            pltpu.VMEM((2, size, half), F32),
+            pltpu.VMEM((rows, 128), F32),
+            pltpu.VMEM((rows, 128), F32),
+            pltpu.VMEM((levels, 2, rows, 128), F32),
+            pltpu.VMEM((2, size + 8, 128), F32),
+            pltpu.VMEM((size + 8, 128), F32),
+            pltpu.VMEM((2, size, 4 * size), BF16),
+            pltpu.SemaphoreType.DMA((5,)),
+            pltpu.SemaphoreType.DMA((2,)),
+            pltpu.SemaphoreType.DMA((levels, 2)),
+            pltpu.SemaphoreType.DMA((2,)),
+            pltpu.SemaphoreType.DMA((2,)),
+            pltpu.SemaphoreType.DMA((3,)),
+            pltpu.SemaphoreType.DMA((3,)),
+        ],
+        compiler_params=pltpu.CompilerParams(
+            collective_id=0, has_side_effects=True, vmem_limit_bytes=48 << 20
+        ),
+        name="tree_reduction",
+    )(bond_factor, tile_mask, potential, injection)
+
+
+def per_device(slabs, bond_factor, tile_mask, potential, injection):
+    amplitude, flag = tree_path(slabs, bond_factor, tile_mask, potential, injection)
+    return lax.cond(
+        flag[0, 0] == 0.0,
+        lambda *operands: amplitude,
+        direct_path,
+        bond_factor,
+        tile_mask,
+        potential,
+        injection,
+    )
+
+
 def solution(mesh):
     in_specs = (
         P("slab", None, None, None),
@@ -121,5 +573,9 @@
     )
     out_specs = P("slab", None, None, "rhs")
     return jax.shard_map(
-        per_device, mesh=mesh, in_specs=in_specs, out_specs=out_specs, check_vma=False
-    )
+        functools.partial(per_device, mesh.shape["slab"]),
+        mesh=mesh,
+        in_specs=in_specs,
+        out_specs=out_specs,
+        check_vma=False,
+    )

time: 1480 us -> 237 us (0.16)
  other arithmetic: 981 us -> 0 us
  Pallas kernels: 0 us -> 230 us
  waiting for transfers between devices: 181 us -> 0 us
  local copies, waits for them, and re-layouts: 92 us -> 3.98 us
  matrix products: 84.3 us -> 0 us
  starting transfers between devices: 58.6 us -> 0 us
  blocking collectives: 42.8 us -> 0 us
  between operations: 25 us -> 0.73 us
    another operation x194 -> x0, other arithmetic: 956 us -> none  [the longest x119 637 us: apply_inverse(): factor_low = jnp.linalg.cholesky(real_form(block))]
    pallas_call x0 -> x1, Pallas kernels: none -> 230 us  [tree_path(): pl.pallas_call(functools.partial(tree_kernel, slabs), out_shape=(jax.Shap...]
    ppermute x15 -> x0, waiting for transfers between devices: 181 us -> none  [passed_along(): return lax.ppermute(array, axis, pairs)]
    another operation x137 -> x0, local copies, waits for them, and re-layouts: 70.7 us -> none  [the longest x93 61.6 us: solve_stacked(): lax.linalg.triangular_solve(factor_low, forward_part, left_side=True, low...]
    another operation x160 -> x0, matrix products: 59 us -> none  [the longest x56 21.5 us: solve_stacked(): lax.linalg.triangular_solve(factor_low, stacked, left_side=True, lower=True)]
    ppermute x15 -> x0, starting transfers between devices: 58.6 us -> none  [passed_along(): return lax.ppermute(array, axis, pairs)]
    all_gather x19 -> x0, blocking collectives: 42.8 us -> none  [the longest x7 16.7 us: per_device(): lax.all_gather(diag_change, 'rhs', axis=2, tiled=True)]
    dot_general x60 -> x0, matrix products: 25.3 us -> none  [the longest x56 23.6 us: transposed_product(): lax.dot_general(operand, other, (((0,), (0,)), ((), ())), precision=PRECISE)]
  transfers between devices with their start and end apart: 15 -> 0, of which waited for: 14 -> 0; matrix products, arithmetic and copies ran while one was open for 1% -> 0% of each run, Pallas kernels for 0% -> 0%
where the time goes in v1:
time: 237 us; the launch traced here: 234 us
  Pallas kernels  230 us (97%)
  local copies, waits for them, and re-layouts  3.98 us (2%)
    pallas_call x1, Pallas kernels, tree_path(): pl.pallas_call(functools.partial(tree_kernel, slabs), out_shape=(jax.Shap...  230 us

profile of v1, /device:TPU:42, one launch (start us, length us, event | category | flops | bytes accessed | tf_op | source)
XLA Modules:
  0.0 234.5 jit_solution(8071921981854858159)
XLA Ops:
  0.0 0.0 copy-start.2
  0.0 1.1 copy.153.injection_ref
  1.1 0.0 copy-start.3
  1.1 229.8 %tree_reduction.1 = (f32[1,2,256,64]{3,2,1,0:T(8,128)}, f32[8,128]{1,0:T(8,128)S(1)}) custom-call(f32[1,2,256,256]{3,2,1,0:T(8,128)} %factor_ref.1, s32[1,4,4]{2,1,0:T(4,128)} %mask_ref.1, f32[1,256]{1,0:T(1,128)} %potential_ref.1, f32[1,2,256,64]{3,2,1,0:T(8,128)S(1)} %copy.153.injection_ref), custom_call_target="tpu_custom_call" | custom-call | tf_op jit(solution)/shard_map/tree_reduction/pallas_call | solution.py:518
  230.9 0.5 slice.853
  232.1 0.0 copy-start.38
  232.1 0.0 copy-start.39
  232.1 0.0 copy-done.2
  232.1 0.0 copy-done.3
  232.1 0.6 copy-done.38
  232.8 0.0 copy-done.39
  232.8 1.1 conditional.1
  232.8 1.1 copy.154
  233.8 0.0 copy-start.37
  233.8 0.6 copy-done.37
Async XLA Ops:
  0.0 232.1 %copy-start.2 = (f32[1,2,256,256]{3,2,1,0:T(8,128)S(1)}, f32[1,2,256,256]{3,2,1,0:T(8,128)}, u32[]{:S(2)}) copy-start(f32[1,2,256,256]{3,2,1,0:T(8,128)} %factor_ref.1) | copy-start | bytes 1572868
  1.1 231.0 %copy-start.3 = (f32[1,2,256,64]{2,3,1,0:T(8,128)S(1)}, f32[1,2,256,64]{2,3,1,0:T(8,128)}, u32[]{:S(2)}) copy-start(f32[1,2,256,64]{2,3,1,0:T(8,128)} %param.14) | copy-start | bytes 393220
  232.1 0.7 copy-start.38
  232.1 0.7 copy-start.39
  233.8 0.7 copy-start.37

commit v2 on v1

--- a/solution.py
+++ b/solution.py
@@ -148,12 +148,21 @@
     out_ref,
     flag_ref,
     ground,
-    coupling,
+    links,
+    matrix,
+    spare,
     waves,
     flag,
     bond_out,
-    near_bond,
-    near_out,
+    bond_in,
+    corner_out,
+    corner_in,
+    ground_out,
+    ground_in,
+    waves_out,
+    waves_in,
+    link_out,
+    link_in,
     far_out,
     terms_in,
     wave_in,
@@ -161,6 +170,10 @@
     back,
     send_sem,
     bond_sem,
+    corner_sem,
+    ground_sem,
+    waves_sem,
+    link_sem,
     terms_sem,
     wave_sem,
     wave_send_sem,
@@ -182,14 +195,24 @@
         even = jnp.where(position % (1 << k) == 0, 1, 0)
         level = level + even
         stride = stride + even * (1 << (k - 1))
-    is_root = position == 0
     not_root = position > 0
+    inner = level > 0
+    inner_left = jnp.logical_and(inner, not_root)
+    deep = level > 1
+    deep_left = jnp.logical_and(deep, not_root)
+    shallow = position % 4 != 0
     has_right = jnp.logical_and(not_root, position + stride < slabs)
     near_is_right = jnp.logical_and(has_right, (position // stride) % 4 == 1)
     near = jnp.where(near_is_right, 1, 0)
     far = 1 - near
     near_target = jnp.where(near_is_right, position + stride, position - stride)
     far_target = jnp.where(near_is_right, position - stride, position + stride)
+    near_is_root = near_target == 0
+    sends_ground = jnp.logical_and(not_root, jnp.logical_not(near_is_root))
+    sends_link = jnp.logical_and(
+        has_right, jnp.logical_or((far_target // stride) % 8 == 4, jnp.logical_and(far_target == 0, stride * 4 == slabs))
+    )
+    sends_bond = (position + 1) % 4 != 0
 
     def remote(source, target, sent, received, slab_to, core_to):
         return pltpu.make_async_remote_copy(
@@ -201,6 +224,25 @@
             device_id_type=MESH,
         )
 
+    def arrival(block, received):
+        return remote(block, block, send_sem.at[1], received, position, twin)
+
+    def join(block, which):
+        return remote(block, block, join_send_sem.at[which], join_sem.at[which], position, twin)
+
+    row = lax.broadcasted_iota(jnp.int32, (size, half), 0)
+    lane_half = lax.broadcasted_iota(jnp.int32, (size, half), 1)
+    column = lane_half + core * half
+    square_row = lax.broadcasted_iota(jnp.int32, (size, size), 0)
+    square_column = lax.broadcasted_iota(jnp.int32, (size, size), 1)
+    own_real = pl.ds(pl.multiple_of(core * half, half), half)
+    own_imag = pl.ds(pl.multiple_of(core * half + size, half), half)
+
+    for h in range(2):
+        energies = jnp.broadcast_to(potential_ref[:, h * half : (h + 1) * half], (size, half))
+        ground[h, 0] = jnp.where(row == lane_half + h * half, energies, 0.0)
+        ground[h, 1] = jnp.zeros((size, half), F32)
+
     barrier = pltpu.get_barrier_semaphore()
 
     def greet(slab_to, core_to):
@@ -215,6 +257,29 @@
         pl.when(jnp.logical_and(level >= k, position >= step))(
             functools.partial(greet, position - step, core)
         )
+
+    def turn(value):
+        width = value.shape[1] // 2
+        return jnp.concatenate([-value[:, width:], value[:, :width]], 1)
+
+    def expand(value):
+        return jnp.concatenate([value, turn(value)], 0)
+
+    def adjoint_of(value):
+        return jnp.concatenate([value[:, :size].T, -value[:, size:].T], 1)
+
+    def unpack(square):
+        turned = square.T
+        real = jnp.where(square_row >= square_column, square, turned)
+        below = jnp.where(square_row > square_column, -turned, 0.0)
+        imag = jnp.where(square_row < square_column, square, below)
+        return jnp.concatenate([real, imag], 1)
+
+    def both_halves(block):
+        return jnp.concatenate([block[0], block[1]], 1)
+
+    def whole(block):
+        return jnp.concatenate([block[0, 0], block[1, 0], block[0, 1], block[1, 1]], 1)
 
     lane = lax.broadcasted_iota(jnp.int32, (1, 128), 1)
     masked = []
@@ -231,53 +296,14 @@
                 blocks.append(piece * keep)
             rows.append(jnp.concatenate(blocks, 1))
         masked.append(jnp.concatenate(rows, 0))
-    left = split(jnp.concatenate(masked, 1))
-    turned = [masked[0].T, -masked[1].T]
-    right = pair_map(
-        lambda planes: planes,
-        split(
-            jnp.concatenate(
-                [jnp.concatenate(turned, 1), jnp.concatenate([-turned[1], turned[0]], 1)], 0
-            )
-        ),
-    )
-    bond = dot3(left, right)
-
-    def store_halves(store, value):
-        for h in range(2):
-            for plane in range(2):
-                store(h, plane, value[:, plane * size + h * half : plane * size + (h + 1) * half])
-
-    def keep_out(h, plane, value):
-        bond_out[h, plane] = value
-
-    store_halves(keep_out, bond)
-
-    row = lax.broadcasted_iota(jnp.int32, (size, half), 0)
-    column = lax.broadcasted_iota(jnp.int32, (size, half), 1) + core * half
-    own = jnp.where(
-        core == 0, potential_ref[:, 0:half], potential_ref[:, half:size]
-    )
-    ground[core, 0] = jnp.where(row == column, jnp.broadcast_to(own, (size, half)), 0.0)
-    ground[core, 1] = jnp.zeros((size, half), F32)
+    factor = jnp.concatenate(masked, 1)
+    bond = dot3(split(factor), pair_map(expand, split(adjoint_of(factor))))
+    packed = jnp.where(square_row >= square_column, bond[:, :size], bond[:, size:])
+    bond_out[0] = packed[:, :half]
+    bond_out[1] = packed[:, half:]
+
     waves[...] = jnp.concatenate([injection_ref[0, 0], injection_ref[0, 1]], 1)
     flag[...] = jnp.zeros_like(flag)
-
-    @pl.when(jnp.logical_not(has_right))
-    def _():
-        coupling[1] = jnp.zeros((2, 2, size, half), F32)
-
-    @pl.when(is_root)
-    def _():
-        coupling[0] = jnp.zeros((2, 2, size, half), F32)
-
-    @pl.when(position == slabs - 1)
-    def _():
-        ground[core] = ground[core] + bond_out[core]
-
-    @pl.when(jnp.logical_and(level == 0, has_right))
-    def _():
-        coupling[1] = bond_out[...]
 
     partners = jnp.int32(1)
     for k in range(levels):
@@ -288,78 +314,87 @@
 
     def bond_copy():
         return remote(
-            bond_out.at[core],
-            coupling.at[0, core],
-            send_sem.at[0],
-            bond_sem.at[0],
-            position + 1,
-            core,
-        )
-
-    pl.when(level > 0)(lambda: bond_copy().start())
-
-    def terms_arrival(k, side):
-        return remote(
-            terms_in.at[k, side], terms_in.at[k, side], send_sem.at[1], terms_sem.at[k, side], position, twin
-        )
+            bond_out.at[core], bond_in.at[core], send_sem.at[0], bond_sem.at[0], position + 1, core
+        )
+
+    pl.when(sends_bond)(lambda: bond_copy().start())
+
+    @pl.when(shallow)
+    def _():
+        arrival(bond_in.at[core], bond_sem.at[0]).wait_recv()
+        join(bond_in.at[core], 0).start()
+        own_bond = unpack(both_halves(bond_out))
+
+        @pl.when(position < slabs - 1)
+        def _():
+            links[1] = own_bond
+
+        @pl.when(position == slabs - 1)
+        def _():
+            for h in range(2):
+                for plane in range(2):
+                    first = plane * size + h * half
+                    ground[h, plane] += own_bond[:, first : first + half]
+            links[1] = jnp.zeros((size, 2 * size), F32)
+
+        join(bond_in.at[twin], 0).wait_recv()
+        links[0] = unpack(both_halves(bond_in))
 
     def add_terms(k, side):
-        terms_arrival(k, side).wait_recv()
+        arrival(terms_in.at[k, side], terms_sem.at[k, side]).wait_recv()
         ground[core, 0] += terms_in[k, side, 0:size]
         ground[core, 1] += terms_in[k, side, size : 2 * size]
         waves[...] += terms_in[k, side, 2 * size : 3 * size]
         flag[...] = jnp.maximum(flag[...], terms_in[k, side, 3 * size : 3 * size + 8])
 
-    def add_level(k):
+    @pl.loop(0, jnp.maximum(level - 1, 0))
+    def _(k):
         pl.when(not_root)(functools.partial(add_terms, k, 0))
         add_terms(k, 1)
 
-    @pl.loop(0, jnp.maximum(level - 1, 0))
-    def _(k):
-        add_level(k)
-
-    def join(block, which):
-        return remote(block, block, join_send_sem.at[which], join_sem.at[which], position, twin)
-
-    @pl.when(not_root)
-    def _():
-        remote(
-            coupling.at[0, core], coupling.at[0, core], send_sem.at[1], bond_sem.at[0], position, twin
-        ).wait_recv()
-        join(coupling.at[0, core], 0).start()
-
-    two_sided = jnp.logical_and(level > 0, has_right)
-
-    @pl.when(two_sided)
-    def _():
-        remote(
-            coupling.at[1, core], coupling.at[1, core], send_sem.at[1], bond_sem.at[1], position, twin
-        ).wait_recv()
-        join(coupling.at[1, core], 1).start()
-
-    pl.when(level > 0)(lambda: add_level(level - 1))
-    join(ground.at[core], 2).start()
-    pl.when(not_root)(lambda: join(coupling.at[0, twin], 0).wait_recv())
-    pl.when(two_sided)(lambda: join(coupling.at[1, twin], 1).wait_recv())
-    join(ground.at[twin], 2).wait_recv()
-
-    def whole(block):
-        return jnp.concatenate([block[0, 0], block[1, 0], block[0, 1], block[1, 1]], 1)
-
-    def turn(value):
-        width = value.shape[1] // 2
-        return jnp.concatenate([-value[:, width:], value[:, :width]], 1)
-
-    def expand(value):
-        return jnp.concatenate([value, turn(value)], 0)
-
-    matrix = whole(ground) + whole(coupling.at[0]) + whole(coupling.at[1])
+    pl.when(inner)(lambda: join(ground.at[core], 5).start())
+
+    def link_arrival(side):
+        arrival(link_in.at[side, core], link_sem.at[side]).wait_recv()
+        join(link_in.at[side, core], 6 + side).start()
+
+    def link_whole(side):
+        join(link_in.at[side, twin], 6 + side).wait_recv()
+        links[side] = adjoint_of(whole(link_in.at[side]))
+
+    pl.when(deep_left)(functools.partial(link_arrival, 0))
+    pl.when(deep)(functools.partial(link_arrival, 1))
+    pl.when(deep_left)(functools.partial(link_whole, 0))
+    pl.when(deep)(functools.partial(link_whole, 1))
+
+    @pl.when(jnp.logical_not(not_root))
+    def _():
+        links[0] = jnp.zeros((size, 2 * size), F32)
+
+    pl.when(inner)(lambda: join(ground.at[twin], 5).wait_recv())
+    matrix[...] = whole(ground) + links[0] + links[1]
+
+    def corner_arrival(side):
+        arrival(corner_in.at[side, core], corner_sem.at[side]).wait_recv()
+        join(corner_in.at[side, core], 1 + side).start()
+
+    def corner_whole(side):
+        join(corner_in.at[side, twin], 1 + side).wait_recv()
+        term = unpack(both_halves(corner_in.at[side]))
+        matrix[...] -= term
+        links[side] -= term
+
+    pl.when(inner_left)(functools.partial(corner_arrival, 0))
+    pl.when(inner)(functools.partial(corner_arrival, 1))
+    pl.when(inner_left)(functools.partial(corner_whole, 0))
+    pl.when(inner)(functools.partial(corner_whole, 1))
+
     wide_row = lax.broadcasted_iota(jnp.int32, (size, 2 * size), 0)
     wide_column = lax.broadcasted_iota(jnp.int32, (size, 2 * size), 1)
     unit = jnp.where(wide_row == wide_column, 1.0, 0.0).astype(F32)
-    mean = jnp.sum(matrix * unit, keepdims=True) / size
+    mean = jnp.sum(matrix[...] * unit, keepdims=True) / size
     scale = 1.0 / mean
-    scaled = matrix * scale
+    scaled = matrix[...] * scale
     power = unit - scaled
     inverse = unit + power
     power = power.astype(BF16)
@@ -369,107 +404,132 @@
         inverse = inverse + both[:size]
         power = both[size:].astype(BF16)
     inverse = inverse + dot(inverse.astype(BF16), expand(power))
-    residual = unit - dot3(split(scaled), pair_map(expand, split(inverse)))
-    inverse = inverse + dot(inverse.astype(BF16), expand(residual.astype(BF16)))
+    inverse_pair = split(inverse)
+    residual = unit - dot3(split(scaled), pair_map(expand, inverse_pair))
+    inverse = inverse + dot3(inverse_pair, pair_map(expand, split(residual)))
     squared = jnp.sum(residual * residual, keepdims=True)
     bad = jnp.where(squared < RESIDUAL_LIMIT, 0.0, 1.0)
     flag[...] = jnp.maximum(flag[...], jnp.broadcast_to(bad, (8, 128)))
     solver = split(inverse * scale)
 
-    def turn_waves(value):
-        return jnp.concatenate([-value[:, cols:], value[:, :cols]], 1)
-
-    def expand_waves(value):
-        return jnp.concatenate([value, turn_waves(value)], 0)
-
-    solved_waves = dot3(solver, pair_map(expand_waves, split(waves[...])))
-
-    def own_half(block):
-        return jnp.concatenate([block[core, 0], block[core, 1]], 1)
-
-    near_copy_bond = remote(
-        near_bond,
-        coupling.at[far, core],
+    def ground_arrival(side):
+        arrival(ground_in.at[side, core], ground_sem.at[side]).wait_recv()
+        join(ground_in.at[side, core], 3 + side).start()
+
+    def ground_whole(side):
+        join(ground_in.at[side, twin], 3 + side).wait_recv()
+        links[side] -= whole(ground_in.at[side])
+        ground[core] += ground_in[side, core]
+
+    pl.when(inner_left)(functools.partial(ground_arrival, 0))
+    pl.when(inner_left)(functools.partial(ground_arrival, 1))
+    pl.when(inner)(lambda: join(ground.at[core], 5).wait_send())
+    pl.when(inner_left)(functools.partial(ground_whole, 0))
+    pl.when(inner_left)(functools.partial(ground_whole, 1))
+
+    @pl.when(jnp.logical_not(has_right))
+    def _():
+        links[1] = jnp.zeros((size, 2 * size), F32)
+
+    corner_copy = remote(
+        corner_out.at[core],
+        corner_in.at[far, core],
         send_sem.at[2],
-        bond_sem.at[far],
+        corner_sem.at[far],
         near_target,
         core,
     )
-    near_copy = remote(
-        near_out,
-        terms_in.at[level, far],
-        send_sem.at[3],
-        terms_sem.at[level, far],
-        near_target,
-        core,
+    ground_copy = remote(
+        ground_out, ground_in.at[far, core], send_sem.at[3], ground_sem.at[far], near_target, core
+    )
+    waves_copy = remote(
+        waves_out, waves_in.at[far], send_sem.at[4], waves_sem.at[far], near_target, core
     )
     far_copy = remote(
-        far_out,
-        terms_in.at[level, near],
-        send_sem.at[4],
-        terms_sem.at[level, near],
-        far_target,
-        core,
-    )
+        far_out, terms_in.at[level, near], send_sem.at[5], terms_sem.at[level, near], far_target, core
+    )
+    link_copy = remote(
+        link_out, link_in.at[near, core], send_sem.at[6], link_sem.at[near], far_target, core
+    )
+
+    def own_half(ref):
+        return jnp.concatenate([ref[:, own_real], ref[:, own_imag]], 1)
+
+    def add_waves(side):
+        arrival(waves_in.at[side], waves_sem.at[side]).wait_recv()
+        waves[...] += waves_in[side, 0:size]
+        flag[...] = jnp.maximum(flag[...], waves_in[side, size : size + 8])
+
+    def solve_waves():
+        pl.when(inner_left)(functools.partial(add_waves, 0))
+        pl.when(inner)(functools.partial(add_waves, 1))
+        solved = dot3(solver, pair_map(expand, split(waves[...])))
+        wave_out[0:size] = solved
+        return pair_map(expand, split(solved))
+
+    @pl.when(jnp.logical_not(not_root))
+    def _():
+        solve_waves()
 
     @pl.when(not_root)
     def _():
-        def adjoint_pair(block):
-            real = jnp.concatenate([block[0, 0], block[1, 0]], 1).T
-            imag = jnp.concatenate([block[0, 1], block[1, 1]], 1).T
-            return split(jnp.concatenate([real, -imag], 1))
-
-        near_left = adjoint_pair(coupling.at[near])
+        near_adjoint = adjoint_of(links[near])
+        near_left = split(near_adjoint)
+        solved = dot3(solver, pair_map(expand, split(own_half(links.at[near]))))
+        solved_near = pair_map(expand, split(solved))
+        product = dot3(near_left, solved_near)
+        corner_out[core] = jnp.where(row >= column, product[:, :half], product[:, half:])
+        corner_copy.start()
+
+        own_ground = jnp.concatenate([ground[core, 0], ground[core, 1]], 1)
+        solved = dot3(solver, pair_map(expand, split(own_ground)))
+        solved_ground = pair_map(expand, split(solved))
+
+        product = dot3(near_left, solved_ground)
+        ground_out[0] = product[:, :half]
+        ground_out[1] = product[:, half:]
+        pl.when(sends_ground)(lambda: ground_copy.start())
+
+        solved_waves = solve_waves()
+        waves_out[0:size] = dot3(near_left, solved_waves)
+        waves_out[size : size + 8] = flag[...]
+        waves_copy.start()
 
         @pl.when(has_right)
         def _():
-            solved = dot3(solver, pair_map(expand, split(own_half(coupling.at[far]))))
-            product = dot3(near_left, pair_map(expand, split(solved)))
-            near_bond[0] = product[:, :half]
-            near_bond[1] = product[:, half:]
-            near_copy_bond.start()
-
-        solved_ground = pair_map(expand, split(dot3(solver, pair_map(expand, split(own_half(ground))))))
-        waves_pair = pair_map(expand_waves, split(solved_waves))
-
-        def fill(out, left_pair):
-            product = dot3(left_pair, solved_ground)
-            out[0:size] = product[:, :half]
-            out[size : 2 * size] = product[:, half:]
-            out[2 * size : 3 * size] = dot3(left_pair, waves_pair)
-            out[3 * size : 3 * size + 8] = flag[...]
-
-        fill(near_out, near_left)
-        near_copy.start()
-
-        @pl.when(has_right)
+            far_left = split(adjoint_of(links[far]))
+            product = dot3(far_left, solved_ground)
+            far_out[0:size] = product[:, :half]
+            far_out[size : 2 * size] = product[:, half:]
+            far_out[2 * size : 3 * size] = dot3(far_left, solved_waves)
+            far_out[3 * size : 3 * size + 8] = flag[...]
+            far_copy.start()
+
+        @pl.when(sends_link)
         def _():
-            fill(far_out, adjoint_pair(coupling.at[far]))
-            far_copy.start()
+            join(corner_out.at[core], 8).start()
+            join(corner_out.at[twin], 8).wait_recv()
+            spare[...] = near_adjoint - unpack(both_halves(corner_out))
+            link_out[0] = spare[:, own_real] - ground_out[0]
+            link_out[1] = spare[:, own_imag] - ground_out[1]
+            link_copy.start()
 
         for side in range(2):
-            spike = split(dot3(solver, pair_map(expand, split(whole(coupling.at[side])))))
+            spike = split(dot3(solver, pair_map(expand, split(links[side]))))
             for part in range(2):
                 back[part, :, side * 2 * size : (side + 1) * 2 * size] = spike[part]
 
-    def wave_arrival(side):
-        return remote(
-            wave_in.at[side], wave_in.at[side], send_sem.at[1], wave_sem.at[side], position, twin
-        )
-
-    wave_out[0:size] = solved_waves
+    def add_side(side):
+        arrival(wave_in.at[side], wave_sem.at[side]).wait_recv()
+        pair = pair_map(expand, split(wave_in[side, 0:size]))
+        spike = (
+            back[0, :, side * 2 * size : (side + 1) * 2 * size],
+            back[1, :, side * 2 * size : (side + 1) * 2 * size],
+        )
+        wave_out[0:size] += dot3(spike, pair)
 
     @pl.when(not_root)
     def _():
-        def add_side(side):
-            wave_arrival(side).wait_recv()
-            pair = pair_map(expand_waves, split(wave_in[side, 0:size]))
-            spike = (
-                back[0, :, side * 2 * size : (side + 1) * 2 * size],
-                back[1, :, side * 2 * size : (side + 1) * 2 * size],
-            )
-            wave_out[0:size] += dot3(spike, pair)
-
         add_side(0)
         flag[...] = jnp.maximum(flag[...], wave_in[0, size : size + 8])
         pl.when(has_right)(functools.partial(add_side, 1))
@@ -497,16 +557,28 @@
     out_ref[0, 1] = wave_out[0:size, cols:]
     flag_ref[...] = flag[...]
 
-    pl.when(level > 0)(lambda: bond_copy().wait_send())
-    pl.when(not_root)(lambda: join(coupling.at[0, core], 0).wait_send())
-    pl.when(two_sided)(lambda: join(coupling.at[1, core], 1).wait_send())
-    join(ground.at[core], 2).wait_send()
-    pl.when(not_root)(lambda: near_copy.wait_send())
-
-    @pl.when(has_right)
-    def _():
-        near_copy_bond.wait_send()
-        far_copy.wait_send()
+    pl.when(sends_bond)(lambda: bond_copy().wait_send())
+    pl.when(shallow)(lambda: join(bond_in.at[core], 0).wait_send())
+    for side in range(2):
+        pl.when(deep_left if side == 0 else deep)(
+            lambda: join(link_in.at[side, core], 6 + side).wait_send()
+        )
+        pl.when(inner_left if side == 0 else inner)(
+            lambda: join(corner_in.at[side, core], 1 + side).wait_send()
+        )
+        pl.when(inner_left)(lambda: join(ground_in.at[side, core], 3 + side).wait_send())
+
+    @pl.when(not_root)
+    def _():
+        corner_copy.wait_send()
+        pl.when(sends_ground)(lambda: ground_copy.wait_send())
+        waves_copy.wait_send()
+        pl.when(has_right)(lambda: far_copy.wait_send())
+
+    @pl.when(sends_link)
+    def _():
+        join(corner_out.at[core], 8).wait_send()
+        link_copy.wait_send()
 
 
 def tree_path(slabs, bond_factor, tile_mask, potential, injection):
@@ -515,6 +587,7 @@
     levels = slabs.bit_length() - 1
     vmem = pl.BlockSpec(memory_space=pltpu.VMEM)
     rows = 3 * size + 8
+    dma = pltpu.SemaphoreType.DMA
     return pl.pallas_call(
         functools.partial(tree_kernel, slabs),
         out_shape=(
@@ -525,27 +598,40 @@
         out_specs=(vmem, vmem),
         scratch_shapes=[
             pltpu.VMEM((2, 2, size, half), F32),
-            pltpu.VMEM((2, 2, 2, size, half), F32),
+            pltpu.VMEM((2, size, 2 * size), F32),
+            pltpu.VMEM((size, 2 * size), F32),
+            pltpu.VMEM((size, 2 * size), F32),
             pltpu.VMEM((size, 128), F32),
             pltpu.VMEM((8, 128), F32),
+            pltpu.VMEM((2, size, half), F32),
+            pltpu.VMEM((2, size, half), F32),
+            pltpu.VMEM((2, size, half), F32),
             pltpu.VMEM((2, 2, size, half), F32),
             pltpu.VMEM((2, size, half), F32),
-            pltpu.VMEM((rows, 128), F32),
+            pltpu.VMEM((2, 2, 2, size, half), F32),
+            pltpu.VMEM((size + 8, 128), F32),
+            pltpu.VMEM((2, size + 8, 128), F32),
+            pltpu.VMEM((2, size, half), F32),
+            pltpu.VMEM((2, 2, 2, size, half), F32),
             pltpu.VMEM((rows, 128), F32),
             pltpu.VMEM((levels, 2, rows, 128), F32),
             pltpu.VMEM((2, size + 8, 128), F32),
             pltpu.VMEM((size + 8, 128), F32),
             pltpu.VMEM((2, size, 4 * size), BF16),
-            pltpu.SemaphoreType.DMA((5,)),
-            pltpu.SemaphoreType.DMA((2,)),
-            pltpu.SemaphoreType.DMA((levels, 2)),
-            pltpu.SemaphoreType.DMA((2,)),
-            pltpu.SemaphoreType.DMA((2,)),
-            pltpu.SemaphoreType.DMA((3,)),
-            pltpu.SemaphoreType.DMA((3,)),
+            dma((7,)),
+            dma((1,)),
+            dma((2,)),
+            dma((2,)),
+            dma((2,)),
+            dma((2,)),
+            dma((levels, 2)),
+            dma((2,)),
+            dma((2,)),
+            dma((9,)),
+            dma((9,)),
         ],
         compiler_params=pltpu.CompilerParams(
-            collective_id=0, has_side_effects=True, vmem_limit_bytes=48 << 20
+            collective_id=0, has_side_effects=True, vmem_limit_bytes=52 << 20
         ),
         name="tree_reduction",
     )(bond_factor, tile_mask, potential, injection)

time: 237 us -> 203 us (0.86)
  Pallas kernels: 230 us -> 196 us
    pallas_call x1, Pallas kernels: 230 us -> 196 us  [tree_path(): pl.pallas_call(functools.partial(tree_kernel, slabs), out_shape=(jax.Shap...]
where the time goes in v2:
time: 203 us; the launch traced here: 201 us
  Pallas kernels  196 us (97%)
  local copies, waits for them, and re-layouts  3.98 us (2%)
    pallas_call x1, Pallas kernels, tree_path(): pl.pallas_call(functools.partial(tree_kernel, slabs), out_shape=(jax.Shap...  196 us

profile of v2, /device:TPU:42, one launch (start us, length us, event | category | flops | bytes accessed | tf_op | source)
XLA Modules:
  0.0 200.8 jit_solution(8876645677583085519)
XLA Ops:
  0.0 0.0 copy-start.2
  0.0 1.1 copy.153.injection_ref
  1.1 0.0 copy-start.3
  1.1 196.1 %tree_reduction.1 = (f32[1,2,256,64]{3,2,1,0:T(8,128)}, f32[8,128]{1,0:T(8,128)S(1)}) custom-call(f32[1,2,256,256]{3,2,1,0:T(8,128)} %factor_ref.1, s32[1,4,4]{2,1,0:T(4,128)} %mask_ref.1, f32[1,256]{1,0:T(1,128)} %potential_ref.1, f32[1,2,256,64]{3,2,1,0:T(8,128)S(1)} %copy.153.injection_ref), custom_call_target="tpu_custom_call" | custom-call | tf_op jit(solution)/shard_map/tree_reduction/pallas_call | solution.py:591
  197.2 0.5 slice.853
  198.3 0.0 copy-start.38
  198.4 0.0 copy-start.39
  198.4 0.0 copy-done.2
  198.4 0.0 copy-done.3
  198.4 0.6 copy-done.38
  199.0 0.0 copy-done.39
  199.0 1.1 conditional.1
  199.0 1.1 copy.154
  200.1 0.0 copy-start.37
  200.1 0.6 copy-done.37
Async XLA Ops:
  0.0 198.4 %copy-start.2 = (f32[1,2,256,256]{3,2,1,0:T(8,128)S(1)}, f32[1,2,256,256]{3,2,1,0:T(8,128)}, u32[]{:S(2)}) copy-start(f32[1,2,256,256]{3,2,1,0:T(8,128)} %factor_ref.1) | copy-start | bytes 1572868
  1.1 197.3 %copy-start.3 = (f32[1,2,256,64]{2,3,1,0:T(8,128)S(1)}, f32[1,2,256,64]{2,3,1,0:T(8,128)}, u32[]{:S(2)}) copy-start(f32[1,2,256,64]{2,3,1,0:T(8,128)} %param.14) | copy-start | bytes 393220
  198.3 0.7 copy-start.38
  198.4 0.7 copy-start.39
  200.1 0.7 copy-start.37

commit v3 on v2

--- a/solution.py
+++ b/solution.py
@@ -160,6 +160,7 @@
     ground_out,
     ground_in,
     waves_out,
+    far_waves_out,
     waves_in,
     link_out,
     link_in,
@@ -182,7 +183,7 @@
 ):
     size = factor_ref.shape[2]
     half = size // 2
-    cols = injection_ref.shape[3]
+    cols = injection_ref.shape[2]
     tile = size // mask_ref.shape[2]
     position = lax.axis_index("slab")
     core = lax.axis_index("rhs")
@@ -302,7 +303,7 @@
     bond_out[0] = packed[:, :half]
     bond_out[1] = packed[:, half:]
 
-    waves[...] = jnp.concatenate([injection_ref[0, 0], injection_ref[0, 1]], 1)
+    waves[...] = jnp.concatenate([injection_ref[0, 0], injection_ref[0, 1]], 0).T
     flag[...] = jnp.zeros_like(flag)
 
     partners = jnp.int32(1)
@@ -342,10 +343,16 @@
 
     def add_terms(k, side):
         arrival(terms_in.at[k, side], terms_sem.at[k, side]).wait_recv()
-        ground[core, 0] += terms_in[k, side, 0:size]
-        ground[core, 1] += terms_in[k, side, size : 2 * size]
-        waves[...] += terms_in[k, side, 2 * size : 3 * size]
-        flag[...] = jnp.maximum(flag[...], terms_in[k, side, 3 * size : 3 * size + 8])
+        ground[core] += terms_in[k, side]
+
+    def add_waves(k, side):
+        arrival(waves_in.at[k, side], waves_sem.at[k, side]).wait_recv()
+        waves[...] += waves_in[k, side, 0:size]
+        flag[...] = jnp.maximum(flag[...], waves_in[k, side, size : size + 8])
+
+    def add_waves_level(k):
+        pl.when(not_root)(functools.partial(add_waves, k, 0))
+        add_waves(k, 1)
 
     @pl.loop(0, jnp.maximum(level - 1, 0))
     def _(k):
@@ -366,6 +373,10 @@
     pl.when(deep)(functools.partial(link_arrival, 1))
     pl.when(deep_left)(functools.partial(link_whole, 0))
     pl.when(deep)(functools.partial(link_whole, 1))
+
+    @pl.loop(0, jnp.maximum(level - 2, 0))
+    def _(k):
+        add_waves_level(k)
 
     @pl.when(jnp.logical_not(not_root))
     def _():
@@ -443,7 +454,20 @@
         ground_out, ground_in.at[far, core], send_sem.at[3], ground_sem.at[far], near_target, core
     )
     waves_copy = remote(
-        waves_out, waves_in.at[far], send_sem.at[4], waves_sem.at[far], near_target, core
+        waves_out,
+        waves_in.at[level, far],
+        send_sem.at[4],
+        waves_sem.at[level, far],
+        near_target,
+        core,
+    )
+    far_waves_copy = remote(
+        far_waves_out,
+        waves_in.at[level, near],
+        send_sem.at[7],
+        waves_sem.at[level, near],
+        far_target,
+        core,
     )
     far_copy = remote(
         far_out, terms_in.at[level, near], send_sem.at[5], terms_sem.at[level, near], far_target, core
@@ -455,14 +479,11 @@
     def own_half(ref):
         return jnp.concatenate([ref[:, own_real], ref[:, own_imag]], 1)
 
-    def add_waves(side):
-        arrival(waves_in.at[side], waves_sem.at[side]).wait_recv()
-        waves[...] += waves_in[side, 0:size]
-        flag[...] = jnp.maximum(flag[...], waves_in[side, size : size + 8])
-
     def solve_waves():
-        pl.when(inner_left)(functools.partial(add_waves, 0))
-        pl.when(inner)(functools.partial(add_waves, 1))
+        @pl.loop(jnp.maximum(level - 2, 0), level)
+        def _(k):
+            add_waves_level(k)
+
         solved = dot3(solver, pair_map(expand, split(waves[...])))
         wave_out[0:size] = solved
         return pair_map(expand, split(solved))
@@ -480,6 +501,7 @@
         product = dot3(near_left, solved_near)
         corner_out[core] = jnp.where(row >= column, product[:, :half], product[:, half:])
         corner_copy.start()
+        pl.when(sends_link)(lambda: join(corner_out.at[core], 8).start())
 
         own_ground = jnp.concatenate([ground[core, 0], ground[core, 1]], 1)
         solved = dot3(solver, pair_map(expand, split(own_ground)))
@@ -490,29 +512,33 @@
         ground_out[1] = product[:, half:]
         pl.when(sends_ground)(lambda: ground_copy.start())
 
-        solved_waves = solve_waves()
-        waves_out[0:size] = dot3(near_left, solved_waves)
-        waves_out[size : size + 8] = flag[...]
-        waves_copy.start()
-
-        @pl.when(has_right)
-        def _():
-            far_left = split(adjoint_of(links[far]))
-            product = dot3(far_left, solved_ground)
-            far_out[0:size] = product[:, :half]
-            far_out[size : 2 * size] = product[:, half:]
-            far_out[2 * size : 3 * size] = dot3(far_left, solved_waves)
-            far_out[3 * size : 3 * size + 8] = flag[...]
-            far_copy.start()
-
         @pl.when(sends_link)
         def _():
-            join(corner_out.at[core], 8).start()
             join(corner_out.at[twin], 8).wait_recv()
             spare[...] = near_adjoint - unpack(both_halves(corner_out))
             link_out[0] = spare[:, own_real] - ground_out[0]
             link_out[1] = spare[:, own_imag] - ground_out[1]
             link_copy.start()
+
+        far_left = split(adjoint_of(links[far]))
+
+        @pl.when(has_right)
+        def _():
+            product = dot3(far_left, solved_ground)
+            far_out[0] = product[:, :half]
+            far_out[1] = product[:, half:]
+            far_copy.start()
+
+        solved_waves = solve_waves()
+        waves_out[0:size] = dot3(near_left, solved_waves)
+        waves_out[size : size + 8] = flag[...]
+        waves_copy.start()
+
+        @pl.when(has_right)
+        def _():
+            far_waves_out[0:size] = dot3(far_left, solved_waves)
+            far_waves_out[size : size + 8] = flag[...]
+            far_waves_copy.start()
 
         for side in range(2):
             spike = split(dot3(solver, pair_map(expand, split(links[side]))))
@@ -553,8 +579,9 @@
         to_right.wait_send()
         pl.when(not_root)(lambda: to_left.wait_send())
 
-    out_ref[0, 0] = wave_out[0:size, :cols]
-    out_ref[0, 1] = wave_out[0:size, cols:]
+    turned_waves = wave_out[0:size].T
+    out_ref[0, 0] = turned_waves[:cols]
+    out_ref[0, 1] = turned_waves[cols:]
     flag_ref[...] = flag[...]
 
     pl.when(sends_bond)(lambda: bond_copy().wait_send())
@@ -573,7 +600,11 @@
         corner_copy.wait_send()
         pl.when(sends_ground)(lambda: ground_copy.wait_send())
         waves_copy.wait_send()
-        pl.when(has_right)(lambda: far_copy.wait_send())
+
+        @pl.when(has_right)
+        def _():
+            far_copy.wait_send()
+            far_waves_copy.wait_send()
 
     @pl.when(sends_link)
     def _():
@@ -586,12 +617,12 @@
     half = size // 2
     levels = slabs.bit_length() - 1
     vmem = pl.BlockSpec(memory_space=pltpu.VMEM)
-    rows = 3 * size + 8
     dma = pltpu.SemaphoreType.DMA
-    return pl.pallas_call(
+    turned = jnp.swapaxes(injection, 2, 3)
+    amplitude, flag = pl.pallas_call(
         functools.partial(tree_kernel, slabs),
         out_shape=(
-            jax.ShapeDtypeStruct(injection.shape, F32),
+            jax.ShapeDtypeStruct(turned.shape, F32),
             jax.ShapeDtypeStruct((8, 128), F32),
         ),
         in_specs=[vmem, pl.BlockSpec(memory_space=pltpu.SMEM), vmem, vmem],
@@ -610,19 +641,20 @@
             pltpu.VMEM((2, size, half), F32),
             pltpu.VMEM((2, 2, 2, size, half), F32),
             pltpu.VMEM((size + 8, 128), F32),
-            pltpu.VMEM((2, size + 8, 128), F32),
+            pltpu.VMEM((size + 8, 128), F32),
+            pltpu.VMEM((levels, 2, size + 8, 128), F32),
             pltpu.VMEM((2, size, half), F32),
             pltpu.VMEM((2, 2, 2, size, half), F32),
-            pltpu.VMEM((rows, 128), F32),
-            pltpu.VMEM((levels, 2, rows, 128), F32),
+            pltpu.VMEM((2, size, half), F32),
+            pltpu.VMEM((levels, 2, 2, size, half), F32),
             pltpu.VMEM((2, size + 8, 128), F32),
             pltpu.VMEM((size + 8, 128), F32),
             pltpu.VMEM((2, size, 4 * size), BF16),
-            dma((7,)),
+            dma((8,)),
             dma((1,)),
             dma((2,)),
             dma((2,)),
-            dma((2,)),
+            dma((levels, 2)),
             dma((2,)),
             dma((levels, 2)),
             dma((2,)),
@@ -634,7 +666,8 @@
             collective_id=0, has_side_effects=True, vmem_limit_bytes=52 << 20
         ),
         name="tree_reduction",
-    )(bond_factor, tile_mask, potential, injection)
+    )(bond_factor, tile_mask, potential, turned)
+    return jnp.swapaxes(amplitude, 2, 3), flag
 
 
 def per_device(slabs, bond_factor, tile_mask, potential, injection):

time: 203 us -> 186 us (0.916)
  Pallas kernels: 196 us -> 180 us
    pallas_call x1, Pallas kernels: 196 us -> 180 us  [tree_path(): pl.pallas_call(functools.partial(tree_kernel, slabs), out_shape=(jax.Shap...]
where the time goes in v3:
time: 186 us; the launch traced here: 183 us
  Pallas kernels  180 us (97%)
  local copies, waits for them, and re-layouts  2.75 us (1%)
    pallas_call x1, Pallas kernels, tree_path(): pl.pallas_call(functools.partial(tree_kernel, slabs), out_shape=(jax.Shap...  180 us

profile of v3, /device:TPU:42, one launch (start us, length us, event | category | flops | bytes accessed | tf_op | source)
XLA Modules:
  0.0 183.0 jit_solution(4204378315324710547)
XLA Ops:
  0.0 0.0 copy-start.2
  0.0 0.0 copy-start.3
  0.0 179.5 %tree_reduction.1 = (f32[1,2,64,256]{3,2,1,0:T(8,128)}, f32[8,128]{1,0:T(8,128)S(1)}) custom-call(f32[1,2,256,256]{3,2,1,0:T(8,128)} %factor_ref.1, s32[1,4,4]{2,1,0:T(4,128)} %mask_ref.1, f32[1,256]{1,0:T(1,128)} %potential_ref.1, f32[1,2,64,256]{3,2,1,0:T(8,128)} %bitcast.1013), custom_call_target="tpu_custom_call" | custom-call | tf_op jit(solution)/shard_map/tree_reduction/pallas_call | solution.py:622
  179.5 0.5 slice.853
  180.7 0.0 copy-start.37
  180.7 0.0 copy-start.38
  180.7 0.0 copy-done.2
  180.7 0.0 copy-done.3
  180.7 0.6 copy-done.37
  181.4 0.0 copy-done.38
  181.4 1.6 copy.281
  (1 shorter events, 0.0 us)
Async XLA Ops:
  0.0 180.7 %copy-start.2 = (f32[1,2,256,256]{3,2,1,0:T(8,128)S(1)}, f32[1,2,256,256]{3,2,1,0:T(8,128)}, u32[]{:S(2)}) copy-start(f32[1,2,256,256]{3,2,1,0:T(8,128)} %factor_ref.1) | copy-start | bytes 1572868
  0.0 180.7 %copy-start.3 = (f32[1,2,256,64]{2,3,1,0:T(8,128)S(1)}, f32[1,2,256,64]{2,3,1,0:T(8,128)}, u32[]{:S(2)}) copy-start(f32[1,2,256,64]{2,3,1,0:T(8,128)} %param.14) | copy-start | bytes 393220
  180.7 0.7 copy-start.37
  180.7 0.7 copy-start.38

commit v4 on v3

--- a/solution.py
+++ b/solution.py
@@ -12,6 +12,7 @@
 F32 = jnp.float32
 BF16 = jnp.bfloat16
 RESIDUAL_LIMIT = 4.0e-4
+PARTS = 4
 
 
 def passed_along(array, axis, by):
@@ -184,6 +185,9 @@
     size = factor_ref.shape[2]
     half = size // 2
     cols = injection_ref.shape[2]
+    part_cols = cols // PARTS
+    part_width = 2 * part_cols
+    part_rows = size // PARTS
     tile = size // mask_ref.shape[2]
     position = lax.axis_index("slab")
     core = lax.axis_index("rhs")
@@ -303,7 +307,14 @@
     bond_out[0] = packed[:, :half]
     bond_out[1] = packed[:, half:]
 
-    waves[...] = jnp.concatenate([injection_ref[0, 0], injection_ref[0, 1]], 0).T
+    waves[...] = jnp.concatenate(
+        [
+            injection_ref[0, plane, p * part_cols : (p + 1) * part_cols]
+            for p in range(PARTS)
+            for plane in range(2)
+        ],
+        0,
+    ).T
     flag[...] = jnp.zeros_like(flag)
 
     partners = jnp.int32(1)
@@ -441,6 +452,7 @@
     @pl.when(jnp.logical_not(has_right))
     def _():
         links[1] = jnp.zeros((size, 2 * size), F32)
+        wave_in[1] = jnp.zeros(wave_in.shape[1:], F32)
 
     corner_copy = remote(
         corner_out.at[core],
@@ -479,14 +491,40 @@
     def own_half(ref):
         return jnp.concatenate([ref[:, own_real], ref[:, own_imag]], 1)
 
+    def turn_waves(value):
+        swapped = jnp.where(
+            lane % part_width < part_cols,
+            -pltpu.roll(value, 128 - part_cols, 1),
+            pltpu.roll(value, part_cols, 1),
+        )
+        return jnp.concatenate([value, swapped], 0)
+
+    def expand_waves(value):
+        high, low = split(value)
+        high_wide, low_wide = high.astype(F32), low.astype(F32)
+        return turn_waves(high_wide).astype(BF16), turn_waves(low_wide).astype(BF16)
+
+    def pack_part(value):
+        packed_part = value[0:part_rows]
+        for q in range(1, PARTS):
+            shifted = pltpu.roll(value[q * part_rows : (q + 1) * part_rows], q * part_width, 1)
+            packed_part = jnp.where(lane >= q * part_width, shifted, packed_part)
+        return packed_part
+
+    def unpack_part(value):
+        pieces = [value]
+        for q in range(1, PARTS):
+            pieces.append(pltpu.roll(value, 128 - q * part_width, 1))
+        return jnp.concatenate(pieces, 0)
+
     def solve_waves():
         @pl.loop(jnp.maximum(level - 2, 0), level)
         def _(k):
             add_waves_level(k)
 
-        solved = dot3(solver, pair_map(expand, split(waves[...])))
-        wave_out[0:size] = solved
-        return pair_map(expand, split(solved))
+        solved = dot3(solver, expand_waves(waves[...]))
+        waves[...] = solved
+        return expand_waves(solved)
 
     @pl.when(jnp.logical_not(not_root))
     def _():
@@ -545,43 +583,68 @@
             for part in range(2):
                 back[part, :, side * 2 * size : (side + 1) * 2 * size] = spike[part]
 
-    def add_side(side):
-        arrival(wave_in.at[side], wave_sem.at[side]).wait_recv()
-        pair = pair_map(expand, split(wave_in[side, 0:size]))
-        spike = (
-            back[0, :, side * 2 * size : (side + 1) * 2 * size],
-            back[1, :, side * 2 * size : (side + 1) * 2 * size],
-        )
-        wave_out[0:size] += dot3(spike, pair)
-
-    @pl.when(not_root)
+    def wave_sends(k, step, p):
+        to_right = remote(
+            wave_out.at[p], wave_in.at[0, p], wave_send_sem.at[0, p], wave_sem.at[0, p], position + step, core
+        )
+        to_left = remote(
+            wave_out.at[p], wave_in.at[1, p], wave_send_sem.at[1, p], wave_sem.at[1, p], position - step, core
+        )
+        return to_right, to_left
+
+    def start_waves(k, step, p):
+        to_right, to_left = wave_sends(k, step, p)
+        to_right.start()
+        pl.when(not_root)(lambda: to_left.start())
+
+    def finish_waves(k, step, p):
+        to_right, to_left = wave_sends(k, step, p)
+        to_right.wait_send()
+        pl.when(not_root)(lambda: to_left.wait_send())
+
+    first_step = jnp.where(inner, stride // 2, 1)
+    rows_flag = pl.ds(part_rows, 8)
+    for p in range(PARTS):
+        own = pltpu.roll(waves[...], 128 - p * part_width, 1) if p else waves[...]
+        wave_out[p, 0:part_rows] = pack_part(own)
+
+        @pl.when(not_root)
+        def _():
+            arrival(wave_in.at[0, p], wave_sem.at[0, p]).wait_recv()
+            pl.when(has_right)(lambda: arrival(wave_in.at[1, p], wave_sem.at[1, p]).wait_recv())
+            sides = [expand_waves(unpack_part(wave_in[side, p, 0:part_rows])) for side in range(2)]
+            pair = [jnp.concatenate([sides[0][e], sides[1][e]], 0) for e in range(2)]
+            total = dot3((back[0], back[1]), pair)
+            wave_out[p, 0:part_rows] += pack_part(total)
+            if p == 0:
+                flag[...] = jnp.maximum(flag[...], wave_in[0, 0, rows_flag])
+
+        wave_out[p, rows_flag] = flag[...]
+        pl.when(inner)(functools.partial(start_waves, level - 1, first_step, p))
+
+    @pl.when(inner)
     def _():
-        add_side(0)
-        flag[...] = jnp.maximum(flag[...], wave_in[0, size : size + 8])
-        pl.when(has_right)(functools.partial(add_side, 1))
-
-    wave_out[size : size + 8] = flag[...]
-
-    @pl.loop(0, level)
+        for p in range(PARTS):
+            finish_waves(level - 1, first_step, p)
+
+    @pl.loop(1, level)
     def _(down):
         k = level - 1 - down
         step = jnp.int32(1)
         for m in range(1, levels):
             step = step + jnp.where(k >= m, 1 << (m - 1), 0)
-        to_right = remote(
-            wave_out, wave_in.at[0], wave_send_sem.at[0], wave_sem.at[0], position + step, core
-        )
-        to_left = remote(
-            wave_out, wave_in.at[1], wave_send_sem.at[1], wave_sem.at[1], position - step, core
-        )
-        to_right.start()
-        pl.when(not_root)(lambda: to_left.start())
-        to_right.wait_send()
-        pl.when(not_root)(lambda: to_left.wait_send())
-
-    turned_waves = wave_out[0:size].T
-    out_ref[0, 0] = turned_waves[:cols]
-    out_ref[0, 1] = turned_waves[cols:]
+        for p in range(PARTS):
+            start_waves(k, step, p)
+        for p in range(PARTS):
+            finish_waves(k, step, p)
+
+    turned_waves = jnp.concatenate(
+        [unpack_part(wave_out[p, 0:part_rows])[:, :part_width] for p in range(PARTS)], 1
+    ).T
+    for p in range(PARTS):
+        for plane in range(2):
+            first = p * part_width + plane * part_cols
+            out_ref[0, plane, p * part_cols : (p + 1) * part_cols] = turned_waves[first : first + part_cols]
     flag_ref[...] = flag[...]
 
     pl.when(sends_bond)(lambda: bond_copy().wait_send())
@@ -647,8 +710,8 @@
             pltpu.VMEM((2, 2, 2, size, half), F32),
             pltpu.VMEM((2, size, half), F32),
             pltpu.VMEM((levels, 2, 2, size, half), F32),
-            pltpu.VMEM((2, size + 8, 128), F32),
-            pltpu.VMEM((size + 8, 128), F32),
+            pltpu.VMEM((2, PARTS, size // PARTS + 8, 128), F32),
+            pltpu.VMEM((PARTS, size // PARTS + 8, 128), F32),
             pltpu.VMEM((2, size, 4 * size), BF16),
             dma((8,)),
             dma((1,)),
@@ -657,8 +720,8 @@
             dma((levels, 2)),
             dma((2,)),
             dma((levels, 2)),
-            dma((2,)),
-            dma((2,)),
+            dma((2, PARTS)),
+            dma((2, PARTS)),
             dma((9,)),
             dma((9,)),
         ],

time: 186 us -> 181 us (0.973); the launches traced: 183 us -> 181 us
  Pallas kernels: 180 us -> 177 us
    pallas_call x1, Pallas kernels: 180 us -> 177 us  [tree_path(): pl.pallas_call(functools.partial(tree_kernel, slabs), out_shape=(jax.Shap...]
where the time goes in v4:
time: 181 us
  Pallas kernels  177 us (98%)
  local copies, waits for them, and re-layouts  2.75 us (2%)
    pallas_call x1, Pallas kernels, tree_path(): pl.pallas_call(functools.partial(tree_kernel, slabs), out_shape=(jax.Shap...  177 us

profile of v4, /device:TPU:42, one launch (start us, length us, event | category | flops | bytes accessed | tf_op | source)
XLA Modules:
  0.0 180.7 jit_solution(3666116000515437511)
XLA Ops:
  0.0 0.0 copy-start.2
  0.0 0.0 copy-start.3
  0.0 177.3 %tree_reduction.1 = (f32[1,2,64,256]{3,2,1,0:T(8,128)}, f32[8,128]{1,0:T(8,128)S(1)}) custom-call(f32[1,2,256,256]{3,2,1,0:T(8,128)} %factor_ref.1, s32[1,4,4]{2,1,0:T(4,128)} %mask_ref.1, f32[1,256]{1,0:T(1,128)} %potential_ref.1, f32[1,2,64,256]{3,2,1,0:T(8,128)} %bitcast.1013), custom_call_target="tpu_custom_call" | custom-call | tf_op jit(solution)/shard_map/tree_reduction/pallas_call | solution.py:685
  177.3 0.5 slice.853
  178.5 0.0 copy-start.37
  178.5 0.0 copy-start.38
  178.5 0.0 copy-done.2
  178.5 0.0 copy-done.3
  178.5 0.6 copy-done.37
  179.2 0.0 copy-done.38
  179.2 1.6 copy.281
  (1 shorter events, 0.0 us)
Async XLA Ops:
  0.0 178.5 %copy-start.2 = (f32[1,2,256,256]{3,2,1,0:T(8,128)S(1)}, f32[1,2,256,256]{3,2,1,0:T(8,128)}, u32[]{:S(2)}) copy-start(f32[1,2,256,256]{3,2,1,0:T(8,128)} %factor_ref.1) | copy-start | bytes 1572868
  0.0 178.5 %copy-start.3 = (f32[1,2,256,64]{2,3,1,0:T(8,128)S(1)}, f32[1,2,256,64]{2,3,1,0:T(8,128)}, u32[]{:S(2)}) copy-start(f32[1,2,256,64]{2,3,1,0:T(8,128)} %param.14) | copy-start | bytes 393220
  178.5 0.7 copy-start.37
  178.5 0.7 copy-start.38

commit v5 on v4

--- a/solution.py
+++ b/solution.py
@@ -534,20 +534,19 @@
     def _():
         near_adjoint = adjoint_of(links[near])
         near_left = split(near_adjoint)
-        solved = dot3(solver, pair_map(expand, split(own_half(links.at[near]))))
-        solved_near = pair_map(expand, split(solved))
-        product = dot3(near_left, solved_near)
-        corner_out[core] = jnp.where(row >= column, product[:, :half], product[:, half:])
+        sources = jnp.concatenate(
+            [links[near, :, own_real], ground[core, 0], links[near, :, own_imag], ground[core, 1]], 1
+        )
+        solved = dot3(solver, pair_map(expand, split(sources)))
+        both_terms = dot3(near_left, pair_map(expand, split(solved)))
+        corner_out[core] = jnp.where(
+            row >= column, both_terms[:, :half], both_terms[:, size : size + half]
+        )
         corner_copy.start()
         pl.when(sends_link)(lambda: join(corner_out.at[core], 8).start())
 
-        own_ground = jnp.concatenate([ground[core, 0], ground[core, 1]], 1)
-        solved = dot3(solver, pair_map(expand, split(own_ground)))
-        solved_ground = pair_map(expand, split(solved))
-
-        product = dot3(near_left, solved_ground)
-        ground_out[0] = product[:, :half]
-        ground_out[1] = product[:, half:]
+        ground_out[0] = both_terms[:, half:size]
+        ground_out[1] = both_terms[:, size + half :]
         pl.when(sends_ground)(lambda: ground_copy.start())
 
         @pl.when(sends_link)
@@ -558,6 +557,10 @@
             link_out[1] = spare[:, own_imag] - ground_out[1]
             link_copy.start()
 
+        solved_ground = pair_map(
+            expand,
+            split(jnp.concatenate([solved[:, half:size], solved[:, size + half :]], 1)),
+        )
         far_left = split(adjoint_of(links[far]))
 
         @pl.when(has_right)
@@ -735,15 +738,11 @@
 
 def per_device(slabs, bond_factor, tile_mask, potential, injection):
     amplitude, flag = tree_path(slabs, bond_factor, tile_mask, potential, injection)
-    return lax.cond(
-        flag[0, 0] == 0.0,
-        lambda *operands: amplitude,
-        direct_path,
-        bond_factor,
-        tile_mask,
-        potential,
-        injection,
-    )
+
+    def direct(state):
+        return jnp.float32(0.0), direct_path(bond_factor, tile_mask, potential, injection)
+
+    return lax.while_loop(lambda state: state[0] > 0.0, direct, (flag[0, 0], amplitude))[1]
 
 
 def solution(mesh):

time: 181 us -> 182 us (level)
  no operation moved by 1% of the time
where the time goes in v5:
time: 182 us
  Pallas kernels  177 us (97%)
  local copies, waits for them, and re-layouts  3.47 us (2%)
    pallas_call x1, Pallas kernels, tree_path(): pl.pallas_call(functools.partial(tree_kernel, slabs), out_shape=(jax.Shap...  177 us

profile of v5, /device:TPU:42, one launch (start us, length us, event | category | flops | bytes accessed | tf_op | source)
XLA Modules:
  0.0 181.6 jit_solution(5779411873256401734)
XLA Ops:
  0.0 0.0 copy-start.38
  0.0 0.7 copy-done.38
  0.7 0.0 copy-start.33
  0.7 177.3 %tree_reduction.1 = (f32[1,2,64,256]{3,2,1,0:T(8,128)}, f32[8,128]{1,0:T(8,128)S(1)}) custom-call(f32[1,2,256,256]{3,2,1,0:T(8,128)} %factor_ref.1, s32[1,4,4]{2,1,0:T(4,128)} %mask_ref.1, f32[1,256]{1,0:T(1,128)S(1)} %copy-done.38, f32[1,2,64,256]{3,2,1,0:T(8,128)} %bitcast.1014), custom_call_target="tpu_custom_call" | custom-call | tf_op jit(solution)/shard_map/tree_reduction/pallas_call | solution.py:688
  178.0 0.5 slice.855
  178.5 0.0 copy-start.37
  178.5 0.0 copy-done.33
  178.5 0.7 copy-done.37
  179.2 0.8 while.9
  180.0 1.6 copy.286
Async XLA Ops:
  0.0 0.7 copy-start.38
  0.7 177.8 %copy-start.33 = (f32[1,2,256,64]{2,3,1,0:T(8,128)S(1)}, f32[1,2,256,64]{2,3,1,0:T(8,128)}, u32[]{:S(2)}) copy-start(f32[1,2,256,64]{2,3,1,0:T(8,128)} %param.14) | copy-start | bytes 393220
  178.5 0.7 copy-start.37

commit v6 on v4

--- a/solution.py
+++ b/solution.py
@@ -645,7 +645,7 @@
         for plane in range(2):
             first = p * part_width + plane * part_cols
             out_ref[0, plane, p * part_cols : (p + 1) * part_cols] = turned_waves[first : first + part_cols]
-    flag_ref[...] = flag[...]
+    flag_ref[...] = flag[0:1, 0:1]
 
     pl.when(sends_bond)(lambda: bond_copy().wait_send())
     pl.when(shallow)(lambda: join(bond_in.at[core], 0).wait_send())
@@ -686,7 +686,7 @@
         functools.partial(tree_kernel, slabs),
         out_shape=(
             jax.ShapeDtypeStruct(turned.shape, F32),
-            jax.ShapeDtypeStruct((8, 128), F32),
+            jax.ShapeDtypeStruct((1, 1), F32),
         ),
         in_specs=[vmem, pl.BlockSpec(memory_space=pltpu.SMEM), vmem, vmem],
         out_specs=(vmem, vmem),

time: 181 us -> 180 us (level)
  no operation moved by 1% of the time
where the time goes in v6:
time: 180 us
  Pallas kernels  177 us (98%)
  local copies, waits for them, and re-layouts  2.24 us (1%)
    pallas_call x1, Pallas kernels, tree_path(): pl.pallas_call(functools.partial(tree_kernel, slabs), out_shape=(jax.Shap...  177 us

profile of v6, /device:TPU:42, one launch (start us, length us, event | category | flops | bytes accessed | tf_op | source)
XLA Modules:
  0.0 180.3 jit_solution(6637436080728996544)
XLA Ops:
  0.0 0.0 copy-start.2
  0.0 0.0 copy-start.3
  0.0 177.3 %tree_reduction.1 = (f32[1,2,64,256]{3,2,1,0:T(8,128)}, f32[1,1]{1,0:T(1,128)}) custom-call(f32[1,2,256,256]{3,2,1,0:T(8,128)} %factor_ref.1, s32[1,4,4]{2,1,0:T(4,128)} %mask_ref.1, f32[1,256]{1,0:T(1,128)} %potential_ref.1, f32[1,2,64,256]{3,2,1,0:T(8,128)} %bitcast.1013), custom_call_target="tpu_custom_call" | custom-call | tf_op jit(solution)/shard_map/tree_reduction/pallas_call | solution.py:685
  178.0 0.0 copy-start.37
  178.0 0.0 copy-start.38
  178.1 0.0 copy-done.2
  178.1 0.0 copy-done.3
  178.1 0.6 copy-done.37
  178.7 0.0 copy-done.38
  178.7 1.6 copy.281
  (1 shorter events, 0.0 us)
Async XLA Ops:
  0.0 178.1 %copy-start.2 = (f32[1,2,256,256]{3,2,1,0:T(8,128)S(1)}, f32[1,2,256,256]{3,2,1,0:T(8,128)}, u32[]{:S(2)}) copy-start(f32[1,2,256,256]{3,2,1,0:T(8,128)} %factor_ref.1) | copy-start | bytes 1572868
  0.0 178.1 %copy-start.3 = (f32[1,2,256,64]{2,3,1,0:T(8,128)S(1)}, f32[1,2,256,64]{2,3,1,0:T(8,128)}, u32[]{:S(2)}) copy-start(f32[1,2,256,64]{2,3,1,0:T(8,128)} %param.14) | copy-start | bytes 393220
  178.0 0.7 copy-start.37
  178.0 0.7 copy-start.38

commit v7 on v5

--- a/solution.py
+++ b/solution.py
@@ -648,7 +648,7 @@
         for plane in range(2):
             first = p * part_width + plane * part_cols
             out_ref[0, plane, p * part_cols : (p + 1) * part_cols] = turned_waves[first : first + part_cols]
-    flag_ref[...] = flag[...]
+    flag_ref[...] = flag[0:1, 0:1]
 
     pl.when(sends_bond)(lambda: bond_copy().wait_send())
     pl.when(shallow)(lambda: join(bond_in.at[core], 0).wait_send())
@@ -689,7 +689,7 @@
         functools.partial(tree_kernel, slabs),
         out_shape=(
             jax.ShapeDtypeStruct(turned.shape, F32),
-            jax.ShapeDtypeStruct((8, 128), F32),
+            jax.ShapeDtypeStruct((1, 1), F32),
         ),
         in_specs=[vmem, pl.BlockSpec(memory_space=pltpu.SMEM), vmem, vmem],
         out_specs=(vmem, vmem),
@@ -738,11 +738,15 @@
 
 def per_device(slabs, bond_factor, tile_mask, potential, injection):
     amplitude, flag = tree_path(slabs, bond_factor, tile_mask, potential, injection)
-
-    def direct(state):
-        return jnp.float32(0.0), direct_path(bond_factor, tile_mask, potential, injection)
-
-    return lax.while_loop(lambda state: state[0] > 0.0, direct, (flag[0, 0], amplitude))[1]
+    return lax.cond(
+        flag[0, 0] == 0.0,
+        lambda *operands: amplitude,
+        direct_path,
+        bond_factor,
+        tile_mask,
+        potential,
+        injection,
+    )
 
 
 def solution(mesh):

time: 182 us -> 180 us (0.989)
  no operation moved by 1% of the time
where the time goes in v7:
time: 180 us
  Pallas kernels  177 us (98%)
  local copies, waits for them, and re-layouts  2.24 us (1%)
    pallas_call x1, Pallas kernels, tree_path(): pl.pallas_call(functools.partial(tree_kernel, slabs), out_shape=(jax.Shap...  177 us

profile of v7, /device:TPU:42, one launch (start us, length us, event | category | flops | bytes accessed | tf_op | source)
XLA Modules:
  0.0 180.3 jit_solution(1484693836702153774)
XLA Ops:
  0.0 0.0 copy-start.2
  0.0 0.0 copy-start.3
  0.0 177.4 %tree_reduction.1 = (f32[1,2,64,256]{3,2,1,0:T(8,128)}, f32[1,1]{1,0:T(1,128)}) custom-call(f32[1,2,256,256]{3,2,1,0:T(8,128)} %factor_ref.1, s32[1,4,4]{2,1,0:T(4,128)} %mask_ref.1, f32[1,256]{1,0:T(1,128)} %potential_ref.1, f32[1,2,64,256]{3,2,1,0:T(8,128)} %bitcast.1013), custom_call_target="tpu_custom_call" | custom-call | tf_op jit(solution)/shard_map/tree_reduction/pallas_call | solution.py:688
  178.1 0.0 copy-start.37
  178.1 0.0 copy-start.38
  178.1 0.0 copy-done.2
  178.1 0.0 copy-done.3
  178.1 0.6 copy-done.37
  178.8 0.0 copy-done.38
  178.8 1.6 copy.281
  (1 shorter events, 0.0 us)
Async XLA Ops:
  0.0 178.1 %copy-start.2 = (f32[1,2,256,256]{3,2,1,0:T(8,128)S(1)}, f32[1,2,256,256]{3,2,1,0:T(8,128)}, u32[]{:S(2)}) copy-start(f32[1,2,256,256]{3,2,1,0:T(8,128)} %factor_ref.1) | copy-start | bytes 1572868
  0.0 178.1 %copy-start.3 = (f32[1,2,256,64]{2,3,1,0:T(8,128)S(1)}, f32[1,2,256,64]{2,3,1,0:T(8,128)}, u32[]{:S(2)}) copy-start(f32[1,2,256,64]{2,3,1,0:T(8,128)} %param.14) | copy-start | bytes 393220
  178.1 0.7 copy-start.37
  178.1 0.7 copy-start.38
